TPU v7x, 256 devices: a whole 4x4x8 slice. The times are simulated.
256 devices in a mesh: phi: 16 (over x_hi, z), row: 4 (over x_lo, core), mass: 4 (over y).
Axes of the slice: x: 4 (x_hi: 2, x_lo: 2; x = x_hi * 2 + x_lo), y: 4, z: 8, core: 2. Of those that a mesh axis runs over, the one named last changes fastest.
Arguments:
- density: float32 [256, 512, 512], P('mass', 'phi', 'row'), may hold values from 0.05 to 1
- cotangent: float32 [256, 512, 512], P('mass', 'phi', 'row'), may hold values from -6 to 6
- drift_in: float32 [256, 512], P('mass'), may hold values from 0.02 to 0.3
- drift_out: float32 [256, 512], P('mass'), may hold values from 0.02 to 0.3
- spread: float32 [256], P('mass'), may hold values from 0.01 to 0.15
- dest_bins: int32 [256], replicated, may hold values from 1 to 254, as said below
- bott_split: float32 [256], replicated, may hold values from 0.05 to 0.95
- coag_rate: float32 [256], replicated, may hold values from 0.05 to 0.3
- frag_pairs: int32 [4, 4], replicated, may hold values from 0 to 1, as said below
- frag_gain: float32 [256, 256], replicated, may hold values from 0.001 to 0.02
- frag_rate: float32 [256], replicated, may hold values from 0.02 to 0.2
- collide_speed: float32 [512, 512], P('phi', 'row'), may hold values from 0.2 to 5
- frag_speed: float32 [512], P('row'), may hold values from 0.5 to 2
- regime: int32 [512, 512], P('phi', 'row'), may hold values 0 or 1
Outputs:
- density_adjoint: float32 [256, 512, 512], P('mass', 'phi', 'row')
- speed_gradient: float32 [512], P('row')
Inputs may be any that keep to these rules, and one draw needn't show every extreme that they name: dest_bins[j] lies between j + 1 and j + 6, but never above 254; dest_bins[0] is 1 and the top bins map to 254. frag_pairs is 1 on the diagonal and in the first row, 0 below the diagonal.
All inputs are finite; a program needn't handle non-finite values. No bound on the sum of `regime` on one device may be relied on, other than what follows from the above.
Results may differ from a plain program's by a relative error of at most 0.000078.
Values sent between devices are 32-bit elements; how exact they have to be, the bound alone decides.
A program may use at most 128 MiB of HBM per device.

v0:
```python
import jax
import jax.numpy as jnp
from jax import lax
from jax.sharding import PartitionSpec as P

RANGE = 64


gate_width = 0.5
highest = lax.Precision.HIGHEST
contract_rows = (((0,), (0,)), ((), ()))


def padded_2(value, sides, width):
    for axis, dim in sides:
        count, length = (lax.axis_size(axis), value.shape[dim])
        up = [(i, (i + 1) % count) for i in range(count)]
        down = [(j, i) for i, j in up]
        last = lax.slice_in_dim(value, length - width, length, axis=dim)
        initial = lax.slice_in_dim(value, 0, width, axis=dim)
        before = lax.ppermute(last, axis, up)
        after = lax.ppermute(initial, axis, down)
        value = jnp.concatenate([before, value, after], axis=dim)
    return value


def coag_matrix(dest_bins, bott_split, coag_rate):
    number = dest_bins.shape[0]
    row_ids = jnp.arange(number, dtype=jnp.int32)[:, None]
    col_ids = jnp.arange(number, dtype=jnp.int32)[None, :]
    target = dest_bins[None, :]
    lower_part = (row_ids == target).astype(jnp.float32) * (1.0 - bott_split)[None, :]
    upper_part = (row_ids == target + 1).astype(jnp.float32) * bott_split[None, :]
    keeper = (row_ids == col_ids).astype(jnp.float32)
    return (lower_part + upper_part - keeper) * coag_rate[None, :]


def frag_matrix(frag_pairs, frag_gain, frag_rate):
    number = frag_gain.shape[0]
    blocks = jnp.repeat(jnp.repeat(frag_pairs, RANGE, axis=0), RANGE, axis=1).astype(jnp.float32)
    row_ids = jnp.arange(number, dtype=jnp.int32)[:, None]
    col_ids = jnp.arange(number, dtype=jnp.int32)[None, :]
    below_diag = (row_ids <= col_ids).astype(jnp.float32)
    keeper = (row_ids == col_ids).astype(jnp.float32)
    return frag_gain * blocks * below_diag - keeper * frag_rate[None, :]


def rimmed(field):
    return padded_2(field, (("phi", 1), ("row", 2)), 1)


def matmul(left, right):
    return jnp.dot(left, right, precision=highest, preferred_element_type=jnp.float32)


def tmatmul(left, right):
    return lax.dot_general(
        left, right, contract_rows, precision=highest, preferred_element_type=jnp.float32
    )


def per_device(
    density,
    cotangent,
    drift_in,
    drift_out,
    spread,
    dest_bins,
    bott_split,
    coag_rate,
    frag_pairs,
    frag_gain,
    frag_rate,
    collide_speed,
    frag_speed,
    regime,
):
    own_bins, azimuth, radial = density.shape
    cell_count = azimuth * radial
    first_bin = lax.axis_index("mass") * own_bins
    row_index = lax.axis_index("row")
    radial_total = radial * lax.axis_size("row")
    coag_full = coag_matrix(dest_bins, bott_split, coag_rate)
    frag_full = frag_matrix(frag_pairs, frag_gain, frag_rate)
    coag_cols = lax.dynamic_slice_in_dim(coag_full, first_bin, own_bins, 1)
    frag_cols = lax.dynamic_slice_in_dim(frag_full, first_bin, own_bins, 1)
    coag_rows = lax.dynamic_slice_in_dim(coag_full, first_bin, own_bins, 0)
    frag_rows = lax.dynamic_slice_in_dim(frag_full, first_bin, own_bins, 0)
    in_pad = jnp.pad(drift_in, ((0, 0), (1, 1)))
    out_pad = jnp.pad(drift_out, ((0, 0), (1, 1)))
    in_ext = lax.dynamic_slice_in_dim(in_pad, row_index * radial, radial + 2, 1)
    out_ext = lax.dynamic_slice_in_dim(out_pad, row_index * radial, radial + 2, 1)
    in_local = in_ext[:, 1:-1]
    out_local = out_ext[:, 1:-1]
    global_rad = row_index * radial + jnp.arange(radial, dtype=jnp.int32)
    in_back = in_local * (global_rad >= 1).astype(jnp.float32)[None, :]
    out_back = out_local * (global_rad <= radial_total - 2).astype(jnp.float32)[None, :]
    center = 1.0 - in_local - out_local - 2.0 * spread[:, None]
    sigma = jax.nn.sigmoid((collide_speed - frag_speed[None, :]) / gate_width)
    flagged = regime.astype(jnp.float32)
    frag_gate = flagged * sigma
    gate_slope = -flagged * sigma * (1.0 - sigma) / gate_width

    def forward_move(field):
        padded = rimmed(field)
        beside_all = padded[:, :-2, 1:-1] + padded[:, 2:, 1:-1]
        return (
            center[:, None, :] * field
            + in_ext[:, None, 2:] * padded[:, 1:-1, 2:]
            + out_ext[:, None, :-2] * padded[:, 1:-1, :-2]
            + spread[:, None, None] * beside_all
        )

    def backward_move(field):
        padded = rimmed(field)
        beside_all = padded[:, :-2, 1:-1] + padded[:, 2:, 1:-1]
        return (
            center[:, None, :] * field
            + in_back[:, None, :] * padded[:, 1:-1, :-2]
            + out_back[:, None, :] * padded[:, 1:-1, 2:]
            + spread[:, None, None] * beside_all
        )

    moved_first = forward_move(density)
    flat_moved = moved_first.reshape(own_bins, cell_count)
    flat_gated = (frag_gate[None] * moved_first).reshape(own_bins, cell_count)
    mixed_first = lax.psum_scatter(
        matmul(coag_cols, flat_moved) + matmul(frag_cols, flat_gated),
        "mass",
        scatter_dimension=0,
        tiled=True,
    )
    state_first = moved_first + mixed_first.reshape(own_bins, azimuth, radial)
    moved_second = forward_move(state_first)

    def adjoint_mass(weight):
        flat_weight = weight.reshape(own_bins, cell_count)
        summed = lax.psum_scatter(
            jnp.stack((tmatmul(coag_rows, flat_weight), tmatmul(frag_rows, flat_weight)), axis=1),
            "mass",
            scatter_dimension=0,
            tiled=True,
        )
        coag_back = summed[:, 0]
        frag_back = summed[:, 1]
        return (
            coag_back.reshape(own_bins, azimuth, radial),
            frag_back.reshape(own_bins, azimuth, radial),
        )

    coag_second, frag_second = adjoint_mass(cotangent)
    weight_second = cotangent + (coag_second + frag_gate[None] * frag_second)
    adjoint_first = backward_move(weight_second)
    coag_first, frag_first = adjoint_mass(adjoint_first)
    weight_first = adjoint_first + (coag_first + frag_gate[None] * frag_first)
    density_adjoint = backward_move(weight_first)
    products = jnp.sum(moved_first * frag_first + moved_second * frag_second, axis=0)
    local_sum = jnp.sum(gate_slope * products, axis=0)
    speed_gradient = lax.psum(local_sum, ("phi", "mass"))
    return (density_adjoint, speed_gradient)


def solution(mesh):
    in_specs = (
        P("mass", "phi", "row"),
        P("mass", "phi", "row"),
        P("mass", None),
        P("mass", None),
        P("mass"),
        P(),
        P(),
        P(),
        P(),
        P(),
        P(),
        P("phi", "row"),
        P("row"),
        P("phi", "row"),
    )
    out_specs = (P("mass", "phi", "row"), P("row"))
    return jax.shard_map(
        per_device, mesh=mesh, in_specs=in_specs, out_specs=out_specs, check_vma=False
    )
```

profile of v0, /device:TPU:8, one launch (start us, length us, event | category | flops | bytes accessed | tf_op | source)
XLA Modules:
  0.0 473.0 jit_solution(18144291337396315812)
XLA Ops:
  11.4 5.1 %convolution_bitcast_fusion.2 = f32[256,1,4096]{2,0,1:T(8,128)S(1)} fusion(f32[8,8,32,128]{3,2,1,0:T(8,128)} %bitcast.58, f32[256,256]{0,1:T(8,128)S(1)} %fusion.45, s32[]{:T(128)S(6)} %select_n.5), kind=kOutput, calls=%fused_computation.4 | convolution fusion | flops 805306368 | bytes 5373956 | tf_op jit(solution)/shard_map/dot_general | solution.py:57
  16.8 3.8 convolution_bitcast_fusion.3
  20.6 3.8 pad_maximum_fusion
  24.5 3.0 copy.246
  28.5 8.3 %collective-permute-start.9 = (f32[64,1,128]{0,1,2:T(1,128)}, f32[64,1,128]{0,1,2:T(1,128)S(1)}, u32[]{:S(2)}, u32[]{:S(2)}) collective-permute-start(f32[64,1,128]{0,1,2:T(1,128)} %get-tuple-element.27), channel_id=1, source_target_pairs={{16,0},{32,16},{48,32},{64,48},{80,64},{96,80},{112,96},{128,112},... | collective-permute-start | bytes 98312 | tf_op jit(solution)/shard_map/ppermute | solution.py:22
  37.7 2.0 pad_dynamic-slice_fusion.3
  39.7 5.4 %collective-permute-done.8 = f32[64,1,128]{0,1,2:T(1,128)S(1)} collective-permute-done((f32[64,1,128]{0,1,2:T(1,128)}, f32[64,1,128]{0,1,2:T(1,128)S(1)}, u32[]{:S(2)}, u32[]{:S(2)}) %collective-permute-start.8) | collective-permute-done | bytes 32800 | tf_op jit(solution)/shard_map/ppermute | solution.py:21
  46.3 1.7 collective-permute-start.10
  50.3 1.5 copy.253
  51.8 1.5 copy.247
  54.8 8.9 %broadcast_multiply_fusion = (f32[64,32,128]{0,1,2:T(8,128)}, f32[64,32,128]{0,1,2:T(8,128)S(1)}) fusion(f32[32,128]{0,1:T(8,128)S(1)} %copy.237, f32[64,1,128]{0,1,2:T(1,128)} %copy-done.23, f32[64,32,128]{0,1,2:T(8,128)} %copy-done.6, f32[64,1,128]{0,1,2:T(1,128)} %copy-done.24, f32[64]{0:T(128)} %param.18, f32[64,34,1]{0,1,2:T(8,128)S(1)} %copy.255, ...), kind=kLoop, calls=%fused_computation.85 | loop fusion | flops 4456448 | bytes 3343616 | tf_op jit(solution)/shard_map/mul | solution.py:126
  63.7 2.5 copy.259
  66.2 4.0 copy.260
  70.3 5.1 %fusion.33 = f32[256,4096]{1,0:T(8,128)S(1)} fusion(f32[8,8,32,128]{3,2,1,0:T(8,128)} %bitcast.68, f32[256,256]{0,1:T(8,128)} %copy-done.11, s32[]{:T(128)S(6)} %select_n.5), kind=kOutput, calls=%fused_computation.74 | convolution fusion | flops 805306368 | bytes 5308420 | tf_op jit(solution)/shard_map/dot_general | solution.py:53
  75.4 5.8 %convolution_add_fusion = f32[256,4096]{1,0:T(8,128)} fusion(f32[256,4096]{1,0:T(8,128)S(1)} %fusion.33, f32[8,8,32,128]{3,2,1,0:T(8,128)S(1)} %bitcast.62, f32[256,256]{0,1:T(8,128)S(1)} %fusion.45, s32[]{:T(128)S(6)} %select_n.5), kind=kOutput, calls=%fused_computation.6 | convolution fusion | flops 806354944 | bytes 9502724 | tf_op jit(solution)/shard_map/dot_general | solution.py:53
  81.7 2.9 copy.240
  84.6 24.7 %reduce-scatter.4.cloned.1.call-done = f32[64,2,4096]{2,0,1:T(8,128)} async-done(((f32[256,2,4096]{2,0,1:T(8,128)}), f32[64,2,4096]{2,0,1:T(8,128)}) %reduce-scatter.4.cloned.1.call-update) | async-done | bytes 2097168 | tf_op jit(solution)/shard_map/reduce_scatter | solution.py:138
  109.3 1.7 slice_bitcast_fusion.2
  111.2 2.9 copy.239
  114.3 2.9 copy.238
  117.2 3.3 add_add_fusion.1
  120.6 5.8 %collective-permute-start.1 = (f32[64,1,128]{0,1,2:T(1,128)S(1)}, f32[64,1,128]{0,1,2:T(1,128)S(1)}, u32[]{:S(2)}, u32[]{:S(2)}) collective-permute-start(f32[64,1,128]{0,1,2:T(1,128)S(1)} %get-tuple-element.33), channel_id=1, source_target_pairs={{16,0},{32,16},{48,32},{64,48},{80,64},{96,80},{112,96},{128,112},... | collective-permute-start | bytes 98312 | tf_op jit(solution)/shard_map/ppermute | solution.py:22
  126.4 1.9 collective-permute-done.1
  128.3 6.0 %collective-permute-done = f32[64,1,128]{0,1,2:T(1,128)S(1)} collective-permute-done((f32[64,1,128]{0,1,2:T(1,128)S(1)}, f32[64,1,128]{0,1,2:T(1,128)S(1)}, u32[]{:S(2)}, u32[]{:S(2)}) %collective-permute-start) | collective-permute-done | bytes 32800 | tf_op jit(solution)/shard_map/ppermute | solution.py:21
  135.9 1.8 collective-permute-done.2
  138.3 4.5 fusion.26
  142.9 3.0 copy.243
  145.9 3.8 convolution_bitcast_fusion
  149.7 3.8 convolution_bitcast_fusion.1
  153.5 3.8 pad_maximum_fusion.1
  157.3 3.7 reduce-scatter.8.cloned.1.call-done
  162.4 2.9 copy.261
  165.3 2.7 add.142
  168.1 6.0 %collective-permute-start.13 = (f32[64,1,128]{0,1,2:T(1,128)S(1)}, f32[64,1,128]{0,1,2:T(1,128)S(1)}, u32[]{:S(2)}, u32[]{:S(2)}) collective-permute-start(f32[64,1,128]{0,1,2:T(1,128)S(1)} %get-tuple-element.25), channel_id=1, source_target_pairs={{16,0},{32,16},{48,32},{64,48},{80,64},{96,80},{112,96},{128,112},... | collective-permute-start | bytes 98312 | tf_op jit(solution)/shard_map/ppermute | solution.py:22
  174.2 1.9 collective-permute-done.13
  176.1 6.0 %collective-permute-done.12 = f32[64,1,128]{0,1,2:T(1,128)S(1)} collective-permute-done((f32[64,1,128]{0,1,2:T(1,128)S(1)}, f32[64,1,128]{0,1,2:T(1,128)S(1)}, u32[]{:S(2)}, u32[]{:S(2)}) %collective-permute-start.12) | collective-permute-done | bytes 32800 | tf_op jit(solution)/shard_map/ppermute | solution.py:21
  182.2 1.8 collective-permute-start.14
  186.6 60.1 %reduce-scatter.6.cloned.1.call-done = f32[64,2,4096]{2,0,1:T(8,128)} async-done(((f32[256,2,4096]{2,0,1:T(8,128)}), f32[64,2,4096]{2,0,1:T(8,128)}) %reduce-scatter.6.cloned.1.call-update) | async-done | bytes 2097168 | tf_op jit(solution)/shard_map/reduce_scatter | solution.py:138
  246.7 2.7 slice_bitcast_fusion
  249.5 2.9 copy.245
  253.9 3.0 copy.244
  257.1 5.9 %add_add_fusion = f32[64,32,128]{0,1,2:T(8,128)S(1)} fusion(f32[64,32,128]{0,1,2:T(8,128)} %copy.245, f32[64,32,128]{0,1,2:T(8,128)} %copy.244, f32[32,128]{0,1:T(8,128)S(1)} %copy.237, f32[64,1,128]{0,1,2:T(1,128)S(1)} %copy-done.18, f32[64,32,128]{0,1,2:T(8,128)S(1)} %add_add_fusion.1, f32[64,1,128]{0,1,2:T(1,128)S(1)} %copy-done.20, f32[64]{0:T(128)} %param.18, ...), kind=kLoop, calls=%fused_computation.70 | loop fusion | flops 4980736 | bytes 4392192 | tf_op jit(solution)/shard_map/add | solution.py:155
  264.5 5.8 %collective-permute-start.5 = (f32[64,1,128]{0,1,2:T(1,128)S(1)}, f32[64,1,128]{0,1,2:T(1,128)S(1)}, u32[]{:S(2)}, u32[]{:S(2)}) collective-permute-start(f32[64,1,128]{0,1,2:T(1,128)S(1)} %get-tuple-element.29), channel_id=1, source_target_pairs={{16,0},{32,16},{48,32},{64,48},{80,64},{96,80},{112,96},{128,112},... | collective-permute-start | bytes 98312 | tf_op jit(solution)/shard_map/ppermute | solution.py:22
  270.4 2.9 fusion.5
  273.3 4.8 %collective-permute-done.4 = f32[64,1,128]{0,1,2:T(1,128)S(1)} collective-permute-done((f32[64,1,128]{0,1,2:T(1,128)S(1)}, f32[64,1,128]{0,1,2:T(1,128)S(1)}, u32[]{:S(2)}, u32[]{:S(2)}) %collective-permute-start.4) | collective-permute-done | bytes 32800 | tf_op jit(solution)/shard_map/ppermute | solution.py:21
  278.8 179.0 %psum.7 = f32[128]{0:T(128)} all-reduce(f32[128]{0:T(128)S(1)} %multiply_reduce_fusion), channel_id=1, replica_groups=mesh['phi'=16,'row'=4,'mass'=4] {'phi','mass'}, use_global_device_ids=true, to_apply=%region_5.6 | all-reduce | flops 128 | bytes 1024 | tf_op jit(solution)/shard_map/psum | solution.py:159
  457.8 4.4 fusion.19
  462.2 3.9 copy.268
  (154 shorter events, 22.4 us)
Async XLA Ops:
  7.2 102.2 %reduce-scatter.4.cloned.1.call-start = ((), (), s32[]{:S(2)}) async-start(), calls=%async_computation.3 | async-start | bytes 10485760 | tf_op jit(solution)/shard_map/reduce_scatter | solution.py:138
  11.4 5.1 %copy-start.40 = (f32[256]{0:T(256)S(1)}, f32[256]{0:T(256)}, u32[]{:S(2)}) copy-start(f32[256]{0:T(256)} %param.20) | copy-start | bytes 3076
  11.4 5.4 %copy-start.9 = (f32[64,32,128]{2,1,0:T(8,128)S(1)}, f32[64,32,128]{2,1,0:T(8,128)}, u32[]{:S(2)}) copy-start(f32[64,32,128]{2,1,0:T(8,128)} %param.15) | copy-start | bytes 3145732
  24.5 136.5 %reduce-scatter.8.cloned.1.call-start = ((), (), s32[]{:S(2)}) async-start(), calls=%async_computation.5 | async-start | bytes 5242880 | tf_op jit(solution)/shard_map/reduce_scatter | solution.py:127
  27.6 26.5 %copy-start.6 = (f32[64,32,128]{0,1,2:T(8,128)}, f32[64,32,128]{0,1,2:T(8,128)S(1)}, u32[]{:S(2)}) copy-start(f32[64,32,128]{0,1,2:T(8,128)S(1)} %copy.246) | copy-start | bytes 3145732
  27.6 20.5 %copy-start.35 = (s32[32,128]{1,0:T(8,128)S(1)}, s32[32,128]{1,0:T(8,128)}, u32[]{:S(2)}) copy-start(s32[32,128]{1,0:T(8,128)} %param.27) | copy-start | bytes 49156
  28.5 11.2 %collective-permute-start.9 = (f32[64,1,128]{0,1,2:T(1,128)}, f32[64,1,128]{0,1,2:T(1,128)S(1)}, u32[]{:S(2)}, u32[]{:S(2)}) collective-permute-start(f32[64,1,128]{0,1,2:T(1,128)} %get-tuple-element.27), channel_id=1, source_target_pairs={{16,0},{32,16},{48,32},{64,48},{80,64},{96,80},{112,96},{128,112},... | collective-permute-start | bytes 98312 | tf_op jit(solution)/shard_map/ppermute | solution.py:22
  36.8 8.3 %collective-permute-start.8 = (f32[64,1,128]{0,1,2:T(1,128)}, f32[64,1,128]{0,1,2:T(1,128)S(1)}, u32[]{:S(2)}, u32[]{:S(2)}) collective-permute-start(f32[64,1,128]{0,1,2:T(1,128)} %get-tuple-element.26), channel_id=1, source_target_pairs={{0,16},{16,32},{32,48},{48,64},{64,80},{80,96},{96,112},{112,128},... | collective-permute-start | bytes 98312 | tf_op jit(solution)/shard_map/ppermute | solution.py:21
  37.0 11.1 %copy-start.36 = (f32[32,128]{1,0:T(8,128)S(1)}, f32[32,128]{1,0:T(8,128)}, u32[]{:S(2)}) copy-start(f32[32,128]{1,0:T(8,128)} %param.25) | copy-start | bytes 49156
  37.0 11.1 %copy-start.42 = (f32[128]{0:T(128)S(1)}, f32[128]{0:T(128)}, u32[]{:S(2)}) copy-start(f32[128]{0:T(128)} %param.26) | copy-start | bytes 1540
  39.6 9.8 %copy-start.23 = (f32[64,1,128]{0,1,2:T(1,128)}, f32[64,1,128]{0,1,2:T(1,128)S(1)}, u32[]{:S(2)}) copy-start(f32[64,1,128]{0,1,2:T(1,128)S(1)} %collective-permute-done.9) | copy-start | bytes 98308
  45.7 7.6 %collective-permute-start.11 = (f32[64,34,1]{0,2,1:T(1,128)}, f32[64,34,1]{0,2,1:T(1,128)}, u32[]{:S(2)}, u32[]{:S(2)}) collective-permute-start(f32[64,34,1]{0,2,1:T(1,128)} %copy.254), channel_id=1, source_target_pairs={{0,4},{4,8},{8,12},{12,0},{1,5},{5,9},{9,13},{13,1},{2,6},{6,10},{... | collective-permute-start | bytes 26120 | tf_op jit(solution)/shard_map/ppermute | solution.py:21
  46.3 7.7 %collective-permute-start.10 = (f32[64,34,1]{0,2,1:T(1,128)}, f32[64,34,1]{0,2,1:T(1,128)}, u32[]{:S(2)}, u32[]{:S(2)}) collective-permute-start(f32[64,34,1]{0,2,1:T(1,128)} %copy.251), channel_id=1, source_target_pairs={{4,0},{8,4},{12,8},{0,12},{5,1},{9,5},{13,9},{1,13},{6,2},{10,6},{... | collective-permute-start | bytes 26120 | tf_op jit(solution)/shard_map/ppermute | solution.py:22
  63.7 6.6 %copy-start = (f32[64,32,128]{0,1,2:T(8,128)}, f32[64,32,128]{0,1,2:T(8,128)S(1)}, u32[]{:S(2)}) copy-start(f32[64,32,128]{0,1,2:T(8,128)S(1)} %get-tuple-element.15) | copy-start | bytes 3145732
  81.3 165.4 %reduce-scatter.6.cloned.1.call-start = ((), (), s32[]{:S(2)}) async-start(), calls=%async_computation.4 | async-start | bytes 10485760 | tf_op jit(solution)/shard_map/reduce_scatter | solution.py:138
  120.5 14.4 %copy-start.30 = (f32[64,128]{1,0:T(8,128)S(1)}, f32[64,128]{1,0:T(8,128)}, u32[]{:S(2)}) copy-start(f32[64,128]{1,0:T(8,128)} %get-tuple-element.40) | copy-start | bytes 98308
  120.5 14.5 %copy-start.29 = (f32[64,128]{1,0:T(8,128)S(1)}, f32[64,128]{1,0:T(8,128)}, u32[]{:S(2)}) copy-start(f32[64,128]{1,0:T(8,128)} %get-tuple-element.37) | copy-start | bytes 98308
  120.5 17.8 %copy-start.38 = (f32[64]{0:T(128)S(1)}, f32[64]{0:T(128)}, u32[]{:S(2)}) copy-start(f32[64]{0:T(128)} %param.18) | copy-start | bytes 772
  120.6 7.7 %collective-permute-start.1 = (f32[64,1,128]{0,1,2:T(1,128)S(1)}, f32[64,1,128]{0,1,2:T(1,128)S(1)}, u32[]{:S(2)}, u32[]{:S(2)}) collective-permute-start(f32[64,1,128]{0,1,2:T(1,128)S(1)} %get-tuple-element.33), channel_id=1, source_target_pairs={{16,0},{32,16},{48,32},{64,48},{80,64},{96,80},{112,96},{128,112},... | collective-permute-start | bytes 98312 | tf_op jit(solution)/shard_map/ppermute | solution.py:22
  126.4 7.9 %collective-permute-start = (f32[64,1,128]{0,1,2:T(1,128)S(1)}, f32[64,1,128]{0,1,2:T(1,128)S(1)}, u32[]{:S(2)}, u32[]{:S(2)}) collective-permute-start(f32[64,1,128]{0,1,2:T(1,128)S(1)} %get-tuple-element.32), channel_id=1, source_target_pairs={{0,16},{16,32},{32,48},{48,64},{64,80},{80,96},{96,112},{112,128},... | collective-permute-start | bytes 98312 | tf_op jit(solution)/shard_map/ppermute | solution.py:21
  128.3 9.4 %copy-start.17 = (f32[64,1,128]{0,1,2:T(1,128)}, f32[64,1,128]{0,1,2:T(1,128)S(1)}, u32[]{:S(2)}) copy-start(f32[64,1,128]{0,1,2:T(1,128)S(1)} %collective-permute-done.1) | copy-start | bytes 98308
  134.3 1.6 collective-permute-start.3
  134.4 3.3 collective-permute-start.2
  168.0 14.0 %copy-start.2 = (f32[64,32,128]{0,1,2:T(8,128)}, f32[64,32,128]{0,1,2:T(8,128)S(1)}, u32[]{:S(2)}) copy-start(f32[64,32,128]{0,1,2:T(8,128)S(1)} %add.142) | copy-start | bytes 3145732
  168.1 7.9 %collective-permute-start.13 = (f32[64,1,128]{0,1,2:T(1,128)S(1)}, f32[64,1,128]{0,1,2:T(1,128)S(1)}, u32[]{:S(2)}, u32[]{:S(2)}) collective-permute-start(f32[64,1,128]{0,1,2:T(1,128)S(1)} %get-tuple-element.25), channel_id=1, source_target_pairs={{16,0},{32,16},{48,32},{64,48},{80,64},{96,80},{112,96},{128,112},... | collective-permute-start | bytes 98312 | tf_op jit(solution)/shard_map/ppermute | solution.py:22
  174.2 7.9 %collective-permute-start.12 = (f32[64,1,128]{0,1,2:T(1,128)S(1)}, f32[64,1,128]{0,1,2:T(1,128)S(1)}, u32[]{:S(2)}, u32[]{:S(2)}) collective-permute-start(f32[64,1,128]{0,1,2:T(1,128)S(1)} %get-tuple-element.24), channel_id=1, source_target_pairs={{0,16},{16,32},{32,48},{48,64},{64,80},{80,96},{96,112},{112,128},... | collective-permute-start | bytes 98312 | tf_op jit(solution)/shard_map/ppermute | solution.py:21
  176.1 73.3 %copy-start.25 = (f32[64,1,128]{0,1,2:T(1,128)}, f32[64,1,128]{0,1,2:T(1,128)S(1)}, u32[]{:S(2)}) copy-start(f32[64,1,128]{0,1,2:T(1,128)S(1)} %collective-permute-done.13) | copy-start | bytes 98308
  182.1 67.3 %copy-start.27 = (f32[64,1,128]{0,1,2:T(1,128)}, f32[64,1,128]{0,1,2:T(1,128)S(1)}, u32[]{:S(2)}) copy-start(f32[64,1,128]{0,1,2:T(1,128)S(1)} %collective-permute-done.12) | copy-start | bytes 98308
  182.1 3.3 collective-permute-start.15
  182.2 3.7 collective-permute-start.14
  257.0 13.3 %copy-start.1 = (f32[64,32,128]{0,1,2:T(8,128)S(1)}, f32[64,32,128]{0,1,2:T(8,128)}, u32[]{:S(2)}) copy-start(f32[64,32,128]{0,1,2:T(8,128)} %copy-done) | copy-start | bytes 3145732
  257.0 13.3 %copy-start.3 = (f32[64,32,128]{0,1,2:T(8,128)S(1)}, f32[64,32,128]{0,1,2:T(8,128)}, u32[]{:S(2)}) copy-start(f32[64,32,128]{0,1,2:T(8,128)} %copy-done.2) | copy-start | bytes 3145732
  257.0 13.3 %copy-start.7 = (f32[64,32,128]{0,1,2:T(8,128)S(1)}, f32[64,32,128]{0,1,2:T(8,128)}, u32[]{:S(2)}) copy-start(f32[64,32,128]{0,1,2:T(8,128)} %copy.238) | copy-start | bytes 3145732
  257.0 13.3 %copy-start.8 = (f32[64,32,128]{0,1,2:T(8,128)S(1)}, f32[64,32,128]{0,1,2:T(8,128)}, u32[]{:S(2)}) copy-start(f32[64,32,128]{0,1,2:T(8,128)} %copy.244) | copy-start | bytes 3145732
  257.0 13.3 %copy-start.21 = (f32[64,128]{0,1:T(8,128)S(1)}, f32[64,128]{0,1:T(8,128)}, u32[]{:S(2)}) copy-start(f32[64,128]{0,1:T(8,128)} %copy.253) | copy-start | bytes 98308
  257.0 13.3 %copy-start.22 = (f32[64,128]{0,1:T(8,128)S(1)}, f32[64,128]{0,1:T(8,128)}, u32[]{:S(2)}) copy-start(f32[64,128]{0,1:T(8,128)} %copy.247) | copy-start | bytes 98308
  257.0 13.3 %copy-start.26 = (f32[64,1,128]{0,1,2:T(1,128)S(1)}, f32[64,1,128]{0,1,2:T(1,128)}, u32[]{:S(2)}) copy-start(f32[64,1,128]{0,1,2:T(1,128)} %copy-done.25) | copy-start | bytes 98308
  257.0 13.3 %copy-start.28 = (f32[64,1,128]{0,1,2:T(1,128)S(1)}, f32[64,1,128]{0,1,2:T(1,128)}, u32[]{:S(2)}) copy-start(f32[64,1,128]{0,1,2:T(1,128)} %copy-done.27) | copy-start | bytes 98308
  257.0 13.3 %copy-start.33 = (f32[64,34,1]{0,1,2:T(8,128)S(1)}, f32[64,34,1]{0,1,2:T(8,128)}, u32[]{:S(2)}) copy-start(f32[64,34,1]{0,1,2:T(8,128)} %copy.265) | copy-start | bytes 26116
  257.1 13.3 %copy-start.34 = (f32[64,34,1]{0,1,2:T(8,128)S(1)}, f32[64,34,1]{0,1,2:T(8,128)}, u32[]{:S(2)}) copy-start(f32[64,34,1]{0,1,2:T(8,128)} %copy.263) | copy-start | bytes 26116
  257.1 13.3 %copy-start.39 = (f32[64]{0:T(128)S(1)}, f32[64]{0:T(128)}, u32[]{:S(2)}) copy-start(f32[64]{0:T(128)} %param.18) | copy-start | bytes 772
  264.5 8.9 %collective-permute-start.5 = (f32[64,1,128]{0,1,2:T(1,128)S(1)}, f32[64,1,128]{0,1,2:T(1,128)S(1)}, u32[]{:S(2)}, u32[]{:S(2)}) collective-permute-start(f32[64,1,128]{0,1,2:T(1,128)S(1)} %get-tuple-element.29), channel_id=1, source_target_pairs={{16,0},{32,16},{48,32},{64,48},{80,64},{96,80},{112,96},{128,112},... | collective-permute-start | bytes 98312 | tf_op jit(solution)/shard_map/ppermute | solution.py:22
  270.3 7.9 %copy-start.5 = (f32[64,32,128]{0,1,2:T(8,128)S(1)}, f32[64,32,128]{0,1,2:T(8,128)}, u32[]{:S(2)}) copy-start(f32[64,32,128]{0,1,2:T(8,128)} %copy-done.4) | copy-start | bytes 3145732
  270.3 7.9 %collective-permute-start.4 = (f32[64,1,128]{0,1,2:T(1,128)S(1)}, f32[64,1,128]{0,1,2:T(1,128)S(1)}, u32[]{:S(2)}, u32[]{:S(2)}) collective-permute-start(f32[64,1,128]{0,1,2:T(1,128)S(1)} %get-tuple-element.28), channel_id=1, source_target_pairs={{0,16},{16,32},{32,48},{48,64},{64,80},{80,96},{96,112},{112,128},... | collective-permute-start | bytes 98312 | tf_op jit(solution)/shard_map/ppermute | solution.py:21
  273.3 5.5 %copy-start.37 = (f32[32,128]{1,0:T(8,128)S(1)}, f32[32,128]{1,0:T(8,128)}, u32[]{:S(2)}) copy-start(f32[32,128]{1,0:T(8,128)} %param.25) | copy-start | bytes 49156
  273.3 5.5 %copy-start.43 = (f32[128]{0:T(128)S(1)}, f32[128]{0:T(128)}, u32[]{:S(2)}) copy-start(f32[128]{0:T(128)} %param.26) | copy-start | bytes 1540
  278.2 179.6 %collective-permute-start.7 = (f32[64,34,1]{0,1,2:T(8,128)S(1)}, f32[64,34,1]{0,1,2:T(8,128)S(1)}, u32[]{:S(2)}, u32[]{:S(2)}) collective-permute-start(f32[64,34,1]{0,1,2:T(8,128)S(1)} %get-tuple-element.21), channel_id=1, source_target_pairs={{4,0},{8,4},{12,8},{0,12},{5,1},{9,5},{13,9},{1,13},{6,2},{10,6},{... | collective-permute-start | bytes 26120 | tf_op jit(solution)/shard_map/ppermute | solution.py:22
  278.2 179.5 %collective-permute-start.6 = (f32[64,34,1]{0,1,2:T(8,128)S(1)}, f32[64,34,1]{0,1,2:T(8,128)S(1)}, u32[]{:S(2)}, u32[]{:S(2)}) collective-permute-start(f32[64,34,1]{0,1,2:T(8,128)S(1)} %get-tuple-element.20), channel_id=1, source_target_pairs={{0,4},{4,8},{8,12},{12,0},{1,5},{5,9},{9,13},{13,1},{2,6},{6,10},{... | collective-permute-start | bytes 26120 | tf_op jit(solution)/shard_map/ppermute | solution.py:21
  (16 other events, 50.6 us)
Sparse Core Ops, SparseCore 0:
  24.6 84.6 reduce-scatter.3
  111.9 49.0 reduce-scatter.7
  163.8 82.8 reduce-scatter.5
where the time goes:
time: 482 us; the launch traced here: 473 us
  blocking collectives  179 us (37%)
  waiting for transfers between devices  118 us (24%)
  local copies, waits for them, and re-layouts  55.3 us (11%)
  other arithmetic  46.7 us (10%)
  starting transfers between devices  31.5 us (7%)
  matrix products  27.3 us (6%)
  between operations  14.9 us (3%)
    psum x1, blocking collectives, per_device(): speed_gradient = lax.psum(local_sum, ('phi', 'mass'))  179 us
    reduce_scatter x2, waiting for transfers between devices, adjoint_mass(): lax.psum_scatter(jnp.stack((tmatmul(coag_rows, flat_weight), tmatmul(frag...  84.8 us
    ppermute x8, starting transfers between devices, padded_2(): after = lax.ppermute(initial, axis, down)  29.6 us
    ppermute x8, waiting for transfers between devices, padded_2(): before = lax.ppermute(last, axis, up)  25.3 us
    unnamed x101, local copies, waits for them, and re-layouts  20.8 us
    dot_general x4, matrix products, tmatmul(): lax.dot_general(left, right, contract_rows, precision=highest, preferred_...  16.4 us
    dot_general x2, matrix products, matmul(): jnp.dot(left, right, precision=highest, preferred_element_type=jnp.float32)  11 us
  transfers between devices with their start and end apart: 19, of which 12 were waited for; matrix products, arithmetic and copies ran while one was open for 18% of the time, Pallas kernels for 0%

commit v1 on v0

v1 whole, which is shorter than its diff:
```python
import functools

import jax
import jax.numpy as jnp
from jax import lax
from jax.experimental import pallas as pl
from jax.experimental.pallas import tpu as pltpu
from jax.sharding import PartitionSpec as P


MESH = pl.DeviceIdType.MESH
F32 = jnp.float32
BF16 = jnp.bfloat16
RANGE = 64
MASS = 4
ROWS = 8
BINS = 256
LANES = 128
GATE_WIDTH = 0.5
BACK, FORTH = 0, 1


def lanes_of(shape):
    return lax.broadcasted_iota(jnp.int32, shape, len(shape) - 1)


def rolled(value, shift):
    shift = shift % LANES
    return value if shift == 0 else pltpu.roll(value, shift, value.ndim - 1)


def swap_blocks(tiles):
    block = lanes_of(tiles[0].shape) // 32
    low = block < 2
    even = block % 2 == 0
    s0, s1, s2, s3 = tiles
    a0 = jnp.where(low, s0, rolled(s2, 64))
    a2 = jnp.where(low, rolled(s0, 64), s2)
    a1 = jnp.where(low, s1, rolled(s3, 64))
    a3 = jnp.where(low, rolled(s1, 64), s3)
    return (
        jnp.where(even, a0, rolled(a1, 32)),
        jnp.where(even, rolled(a0, 96), a1),
        jnp.where(even, a2, rolled(a3, 32)),
        jnp.where(even, rolled(a2, 96), a3),
    )


def high_low(value):
    high = value.astype(BF16)
    return high, (value - high.astype(F32)).astype(BF16)


def kernel(
    pairs,
    density,
    cotangent,
    drift_in,
    drift_out,
    spread,
    dest,
    split,
    rate,
    gain,
    frag_rate,
    speed,
    frag_speed,
    regime,
    out,
    grad,
    raw_c,
    raw_d,
    pack_c,
    pack_d,
    cot,
    dens,
    coef_out,
    coef_in,
    coef,
    back_hi,
    back_lo,
    forth_hi,
    forth_lo,
    gates,
    slopes,
    w2,
    f2,
    a1,
    w1,
    f1,
    m1,
    st,
    res,
    ret,
    edge_out,
    edge_in,
    acc,
    red,
    load_sem,
    field_send,
    field_recv,
    coef_send,
    coef_recv,
    edge_send,
    edge_recv,
    red_send,
    red_recv,
):
    phi = lax.axis_index("phi")
    row = lax.axis_index("row")
    m = lax.axis_index("mass")
    phis = lax.axis_size("phi")
    rows = lax.axis_size("row")
    phi_j = lax.rem(phi, 4)
    phi_i = phi // 4

    load_c = pltpu.make_async_copy(cotangent, raw_c, load_sem.at[0])
    load_d = pltpu.make_async_copy(density, raw_d, load_sem.at[1])
    load_c.start()
    load_d.start()

    def mass_peer(k):
        return {"mass": lax.rem(m + k, MASS)}

    def j_peer(k):
        return {"phi": phi_i * 4 + lax.rem(phi_j + k, 4)}

    def i_peer(k):
        return {"phi": lax.rem(phi_i + k, 4) * 4 + phi_j}

    radial = row * MASS + m
    radials = rows * MASS
    right_at = lax.rem(radial + 1, radials)
    left_at = lax.rem(radial + radials - 1, radials)
    right = {"row": right_at // MASS, "mass": lax.rem(right_at, MASS)}
    left = {"row": left_at // MASS, "mass": lax.rem(left_at, MASS)}
    after = {"phi": lax.rem(phi + 1, phis)}
    before = {"phi": lax.rem(phi + phis - 1, phis)}

    barrier = pltpu.get_barrier_semaphore()
    greeted = (
        [mass_peer(k) for k in (1, 2, 3)]
        + [j_peer(k) for k in (1, 2, 3)]
        + [i_peer(k) for k in (1, 2, 3)]
        + [right, left, after, before]
    )
    for device in greeted:
        pl.semaphore_signal(barrier, inc=1, device_id=device, device_id_type=MESH)

    tile = (RANGE, LANES)
    lane = lanes_of(tile)
    block = lane // 32
    within = lax.rem(lane, 32)
    first = within == 0
    final = within == 31
    at = pl.multiple_of(row * LANES, LANES)
    in_q = drift_in[:, pl.ds(at, LANES)]
    out_q = drift_out[:, pl.ds(at, LANES)]
    square = (RANGE, RANGE)
    on_diag = lax.broadcasted_iota(jnp.int32, square, 0) == lanes_of(square)
    spread_col = jnp.sum(jnp.where(on_diag, jnp.broadcast_to(spread[...], square), 0.0), axis=1, keepdims=True)
    spread_tile = jnp.broadcast_to(spread_col, tile)
    for k in range(MASS):
        coef_out[k] = jnp.where(
            block == 0,
            rolled(in_q, -32 * k),
            jnp.where(block == 1, rolled(out_q, 32 - 32 * k), spread_tile),
        )

    def field_copy(kind, k, ah, source, target):
        return pltpu.make_async_remote_copy(
            src_ref=source,
            dst_ref=target,
            send_sem=field_send.at[kind, k - 1, ah],
            recv_sem=field_recv.at[kind, k - 1, ah],
            device_id=mass_peer(k),
            device_id_type=MESH,
        )

    own = pl.ds(pl.multiple_of(m * RANGE, RANGE), RANGE)

    def cot_copy(k, ah):
        return field_copy(0, k, ah, pack_c.at[lax.rem(m + k, MASS), ah], cot.at[ah, own])

    def dens_copy(k, ah):
        return field_copy(1, k, ah, pack_d.at[lax.rem(m + k, MASS), ah], dens.at[ah + 1, own])

    def ret_copy(k, ah):
        theirs = pl.ds(pl.multiple_of(lax.rem(m + k, MASS) * RANGE, RANGE), RANGE)
        return field_copy(2, k, ah, res.at[ah, theirs], ret.at[m, ah])

    def coef_copy(k):
        return pltpu.make_async_remote_copy(
            src_ref=coef_out.at[lax.rem(m + k, MASS)],
            dst_ref=coef_in.at[own],
            send_sem=coef_send.at[k - 1],
            recv_sem=coef_recv.at[k - 1],
            device_id=mass_peer(k),
            device_id_type=MESH,
        )

    def spread_field(raw, packed, shifted, held, copy):
        flat = raw.reshape(RANGE * 32, LANES)

        def body(ah, carry):
            tiles = swap_blocks([flat[pl.ds(al * 8 + ah, RANGE, stride=32), :] for al in range(4)])
            for k in range(MASS):
                packed[k, ah] = tiles[k]
            for k in (1, 2, 3):
                copy(k, ah).start()
            held[ah + shifted, own] = packed[m, ah]
            return carry

        lax.fori_loop(0, ROWS, body, 0)

    load_c.wait()
    pl.semaphore_wait(barrier, len(greeted))
    spread_field(raw_c, pack_c, 0, cot, cot_copy)
    for k in (1, 2, 3):
        coef_copy(k).start()
    coef_in[own] = coef_out[m]
    load_d.wait()
    spread_field(raw_d, pack_d, 1, dens, dens_copy)

    whole = (BINS, BINS)
    row_ids = lax.broadcasted_iota(jnp.int32, whole, 0)
    col_ids = lanes_of(whole)
    target = jnp.broadcast_to(dest[...], whole)
    upper = jnp.broadcast_to(split[...], whole)
    diag = jnp.where(row_ids == col_ids, 1.0, 0.0)
    coag_full = (
        jnp.where(row_ids == target, 1.0 - upper, 0.0) + jnp.where(row_ids == target + 1, upper, 0.0) - diag
    ) * rate[...]
    strip = (RANGE, BINS)
    strip_block = lanes_of(strip) // RANGE
    chosen = []
    for i in range(MASS):
        line = jnp.zeros(strip, F32)
        for j in range(MASS):
            line = jnp.where(strip_block == j, pairs[i, j].astype(F32), line)
        chosen.append(line)
    chosen = jnp.concatenate(chosen, axis=0)
    frag_full = gain[...] * chosen * jnp.where(row_ids <= col_ids, 1.0, 0.0) - diag * frag_rate[...]
    for at_row, matrix in ((0, coag_full), (BINS, frag_full)):
        hi, lo = high_low(matrix)
        forth_hi[at_row : at_row + BINS] = hi
        forth_lo[at_row : at_row + BINS] = lo
        hi, lo = high_low(matrix.T)
        back_hi[at_row : at_row + BINS] = hi
        back_lo[at_row : at_row + BINS] = lo

    sigma = 1.0 / (1.0 + jnp.exp(-((speed[...] - frag_speed[...]) / GATE_WIDTH)))
    flagged = regime[...].astype(F32)
    gate_all = flagged * sigma
    slope_all = -flagged * sigma * (1.0 - sigma) / GATE_WIDTH
    block8 = lanes_of((ROWS, LANES)) // 32
    for source, kept in ((gate_all, gates), (slope_all, slopes)):
        value = jnp.zeros((ROWS, LANES), F32)
        for al in range(4):
            part = pltpu.roll(source[al * 8 : al * 8 + 8], lax.rem(32 * (al + MASS - m), LANES), 1)
            value = jnp.where(block8 == al, part, value)
        kept[...] = value

    for k in (1, 2, 3):
        coef_copy(k).wait_recv()
    for g in range(MASS):
        bins = slice(g * RANGE, (g + 1) * RANGE)
        turns = [rolled(coef_in[bins], 32 * k) for k in range(4)]

        def everywhere(source):
            value = turns[(0 - source) % 4]
            for b in (1, 2, 3):
                value = jnp.where(block == b, turns[(b - source) % 4], value)
            return value

        c_in, c_out, c_spread = everywhere(0), everywhere(1), everywhere(2)
        coef[0, bins] = c_in
        coef[1, bins] = c_out
        coef[2, bins] = c_spread
        coef[3, bins] = 1.0 - c_in - c_out - 2.0 * c_spread

    has_left = jnp.where(radial > 0, 1.0, 0.0)
    has_right = jnp.where(radial < radials - 1, 1.0, 0.0)

    def edge_copies(n):
        def one(i, device):
            return pltpu.make_async_remote_copy(
                src_ref=edge_out.at[n, i],
                dst_ref=edge_in.at[n, i],
                send_sem=edge_send.at[n, i],
                recv_sem=edge_recv.at[n, i],
                device_id=device,
                device_id_type=MESH,
            )

        return [one(0, right), one(1, left), one(2, after), one(3, before)]

    def send_edges(n, field, way):
        def body(ah, carry):
            last_col, first_col = carry
            for g in range(MASS):
                bins = slice(g * RANGE, (g + 1) * RANGE)
                value = field[ah + 1, bins]
                to_left = value * coef[0, bins] if way == FORTH else value
                to_right = value * coef[1, bins] if way == FORTH else value
                last_col = jnp.where(final, to_right, rolled(last_col, -1))
                first_col = jnp.where(first, to_left, rolled(first_col, 1))
            return last_col, first_col

        zero = jnp.zeros(tile, F32)
        for i in (2, 3):
            value = zero
            for g in range(MASS):
                bins = slice(g * RANGE, (g + 1) * RANGE)
                part = rolled(field[ROWS, bins], 32 * (g - 3)) if i == 2 else rolled(field[1, bins], 32 * g)
                value = jnp.where(block == g, part, value)
            edge_out[n, i] = value
        last_col, first_col = lax.fori_loop(0, ROWS, body, (zero, zero))
        edge_out[n, 0] = last_col
        edge_out[n, 1] = first_col
        for copy in edge_copies(n):
            copy.start()

    def stencil(n, field, way, emit, after_row=None):
        for copy in edge_copies(n):
            copy.wait_recv()
        for g in range(MASS):
            bins = slice(g * RANGE, (g + 1) * RANGE)
            field[0, bins] = jnp.where(
                block == 0, rolled(edge_in[n, 2], -32 * g), rolled(field[ROWS, bins], 32)
            )
            field[ROWS + 1, bins] = jnp.where(
                block == 3, rolled(edge_in[n, 3], 32 * (3 - g)), rolled(field[1, bins], -32)
            )

        def body(ah, carry):
            last_col, first_col = carry
            for g in range(MASS):
                bins = slice(g * RANGE, (g + 1) * RANGE)
                value = field[ah + 1, bins]
                beside = field[ah, bins] + field[ah + 2, bins]
                c_in, c_out = coef[0, bins], coef[1, bins]
                if way == FORTH:
                    outer = jnp.where(final, first_col, rolled(c_in * value, -1))
                    inner = jnp.where(first, last_col, rolled(c_out * value, 1))
                    both = outer + inner
                else:
                    inner = jnp.where(first, last_col, rolled(value, 1))
                    outer = jnp.where(final, first_col, rolled(value, -1))
                    both = c_in * inner + c_out * outer
                emit(ah, g, bins, coef[3, bins] * value + both + coef[2, bins] * beside)
                last_col = rolled(last_col, -1)
                first_col = rolled(first_col, 1)
            if after_row is not None:
                after_row(ah)
            return last_col, first_col

        lax.fori_loop(0, ROWS, body, (edge_in[n, 0] * has_left, edge_in[n, 1] * has_right))

    def mix(source, shifted, hi, lo, state, frags, before_pair=None):
        def body(j, carry):
            ah = 2 * j
            if before_pair is not None:
                before_pair(ah)
                before_pair(ah + 1)
            x = jnp.concatenate([source[ah + shifted], source[ah + shifted + 1]], axis=1)
            x_hi, x_lo = high_low(x)
            y = jnp.dot(hi[...], x_hi, preferred_element_type=F32)
            y += jnp.dot(hi[...], x_lo, preferred_element_type=F32)
            y += jnp.dot(lo[...], x_hi, preferred_element_type=F32)
            gate = jnp.concatenate([gates[pl.ds(ah, 1)], gates[pl.ds(ah + 1, 1)]], axis=1)
            new = x + (y[:BINS] + gate * y[BINS:])
            state[ah + 1] = new[:, :LANES]
            state[ah + 2] = new[:, LANES:]
            if frags is not None:
                frags[ah] = y[BINS:, :LANES]
                frags[ah + 1] = y[BINS:, LANES:]
            return carry

        lax.fori_loop(0, ROWS // 2, body, 0)

    def add_product(ah, value, other):
        summed = jnp.sum((value * other).reshape(RANGE // 8, 8, LANES), axis=0)
        acc[...] += slopes[pl.ds(ah, 1)] * summed

    def arrived(copy):
        def wait(ah):
            for k in (1, 2, 3):
                copy(k, ah).wait_recv()

        return wait

    acc[...] = jnp.zeros((8, LANES), F32)

    mix(cot, 0, back_hi, back_lo, w2, f2, arrived(cot_copy))
    send_edges(0, w2, BACK)

    def keep_a1(ah, g, bins, value):
        a1[ah, bins] = value

    stencil(0, w2, BACK, keep_a1)

    mix(a1, 0, back_hi, back_lo, w1, f1)
    send_edges(1, w1, BACK)

    def wait_dens(ah, carry):
        arrived(dens_copy)(ah)
        return carry

    lax.fori_loop(0, ROWS, wait_dens, 0)
    send_edges(2, dens, FORTH)

    def keep_m1(ah, g, bins, value):
        m1[ah, bins] = value
        add_product(ah, value, f1[ah, bins])

    stencil(2, dens, FORTH, keep_m1)
    mix(m1, 0, forth_hi, forth_lo, st, None)
    send_edges(3, st, FORTH)

    def keep_res(ah, g, bins, value):
        res[ah, bins] = value

    def send_row(ah):
        for k in (1, 2, 3):
            ret_copy(k, ah).start()
        ret[m, ah] = res[ah, own]

    stencil(1, w1, BACK, keep_res, send_row)

    def keep_m2(ah, g, bins, value):
        add_product(ah, value, f2[ah, bins])

    stencil(3, st, FORTH, keep_m2)

    total = jnp.sum(acc[...], axis=0, keepdims=True)
    total = total + rolled(total, 32) + rolled(total, 64) + rolled(total, 96)
    total = jnp.broadcast_to(total, (8, LANES))
    total = jnp.where(block8 == m, total, 0.0)
    for n, (place, peer) in enumerate(((phi_j, j_peer), (phi_i, i_peer), (m, mass_peer))):
        red[n, place] = total
        copies = []
        for k in (1, 2, 3):
            copies.append(
                pltpu.make_async_remote_copy(
                    src_ref=red.at[n, place],
                    dst_ref=red.at[n, place],
                    send_sem=red_send.at[n, k - 1],
                    recv_sem=red_recv.at[n, k - 1],
                    device_id=peer(k),
                    device_id_type=MESH,
                )
            )
        for copy in copies:
            copy.start()
        for copy in copies:
            copy.wait()
        total = (red[n, 0] + red[n, 1]) + (red[n, 2] + red[n, 3])
    grad[...] = total

    flat_out = out.reshape(RANGE * 32, LANES)

    def unpack(ah, carry):
        arrived(ret_copy)(ah)
        tiles = swap_blocks([ret[k, ah] for k in range(MASS)])
        for al in range(4):
            flat_out[pl.ds(al * 8 + ah, RANGE, stride=32), :] = tiles[al]
        return carry

    lax.fori_loop(0, ROWS, unpack, 0)

    def drain(ah, carry):
        for copy in (cot_copy, dens_copy, ret_copy):
            for k in (1, 2, 3):
                copy(k, ah).wait_send()
        return carry

    lax.fori_loop(0, ROWS, drain, 0)
    for k in (1, 2, 3):
        coef_copy(k).wait_send()
    for n in range(4):
        for copy in edge_copies(n):
            copy.wait_send()


def per_device(
    density,
    cotangent,
    drift_in,
    drift_out,
    spread,
    dest_bins,
    bott_split,
    coag_rate,
    frag_pairs,
    frag_gain,
    frag_rate,
    collide_speed,
    frag_speed,
    regime,
):
    vmem = pl.BlockSpec(memory_space=pltpu.VMEM)
    hbm = pl.BlockSpec(memory_space=pl.ANY)
    smem = pl.BlockSpec(memory_space=pltpu.SMEM)
    field = pltpu.VMEM((ROWS, BINS, LANES), F32)
    padded = pltpu.VMEM((ROWS + 2, BINS, LANES), F32)
    packed = pltpu.VMEM((MASS, ROWS, RANGE, LANES), F32)
    raw = pltpu.VMEM(density.shape, F32)
    matrix = pltpu.VMEM((2 * BINS, BINS), BF16)
    small = pltpu.VMEM((ROWS, LANES), F32)
    edges = pltpu.VMEM((4, 4, RANGE, LANES), F32)
    dma = pltpu.SemaphoreType.DMA
    adjoint, gradient = pl.pallas_call(
        kernel,
        out_shape=(
            jax.ShapeDtypeStruct(density.shape, F32),
            jax.ShapeDtypeStruct((ROWS, LANES), F32),
        ),
        in_specs=[smem, hbm, hbm] + [vmem] * 11,
        out_specs=(vmem, vmem),
        scratch_shapes=[
            raw,
            raw,
            packed,
            packed,
            field,
            padded,
            pltpu.VMEM((MASS, RANGE, LANES), F32),
            pltpu.VMEM((BINS, LANES), F32),
            pltpu.VMEM((4, BINS, LANES), F32),
            matrix,
            matrix,
            matrix,
            matrix,
            small,
            small,
            padded,
            field,
            field,
            padded,
            field,
            field,
            padded,
            field,
            packed,
            edges,
            edges,
            small,
            pltpu.VMEM((3, 4, ROWS, LANES), F32),
            dma((2,)),
            dma((3, 3, ROWS)),
            dma((3, 3, ROWS)),
            dma((3,)),
            dma((3,)),
            dma((4, 4)),
            dma((4, 4)),
            dma((3, 3)),
            dma((3, 3)),
        ],
        compiler_params=pltpu.CompilerParams(
            collective_id=0, has_side_effects=True, vmem_limit_bytes=48 << 20
        ),
    )(
        frag_pairs,
        density,
        cotangent,
        drift_in,
        drift_out,
        spread[None, :],
        dest_bins[None, :],
        bott_split[None, :],
        coag_rate[None, :],
        frag_gain,
        frag_rate[None, :],
        collide_speed,
        frag_speed[None, :],
        regime,
    )
    return adjoint, gradient[0]


def solution(mesh):
    in_specs = (
        P("mass", "phi", "row"),
        P("mass", "phi", "row"),
        P("mass", None),
        P("mass", None),
        P("mass"),
        P(),
        P(),
        P(),
        P(),
        P(),
        P(),
        P("phi", "row"),
        P("row"),
        P("phi", "row"),
    )
    out_specs = (P("mass", "phi", "row"), P("row"))
    return jax.shard_map(
        per_device, mesh=mesh, in_specs=in_specs, out_specs=out_specs, check_vma=False
    )
```

time: 482 us -> 90.2 us (0.19); the launches traced: 473 us -> 89.7 us
  blocking collectives: 179 us -> 0 us
  waiting for transfers between devices: 118 us -> 0 us
  Pallas kernels: 0 us -> 80.1 us
  other arithmetic: 46.7 us -> 0 us
  local copies, waits for them, and re-layouts: 55.3 us -> 8.83 us
  starting transfers between devices: 31.5 us -> 0 us
  matrix products: 27.3 us -> 0 us
  between operations: 14.9 us -> 0.71 us
    psum x1 -> x0, blocking collectives: 179 us -> none  [per_device(): speed_gradient = lax.psum(local_sum, ('phi', 'mass'))]
    reduce_scatter x3 -> x0, waiting for transfers between devices: 88.4 us -> none  [the longest x2 84.8 us: adjoint_mass(): lax.psum_scatter(jnp.stack((tmatmul(coag_rows, flat_weight), tmatmul(frag...]
    pallas_call x0 -> x1, Pallas kernels: none -> 80.1 us  [per_device(): pl.pallas_call(kernel, out_shape=(jax.ShapeDtypeStruct(density.shape, F32...]
    ppermute x16 -> x0, starting transfers between devices: 30.9 us -> none  [the longest x8 29.6 us: padded_2(): after = lax.ppermute(initial, axis, down)]
    ppermute x16 -> x0, waiting for transfers between devices: 29.8 us -> none  [the longest x8 25.3 us: padded_2(): before = lax.ppermute(last, axis, up)]
    dot_general x6 -> x0, matrix products: 27.3 us -> none  [the longest x4 16.4 us: tmatmul(): lax.dot_general(left, right, contract_rows, precision=highest, preferred_...]
    add x6 -> x0, other arithmetic: 21.5 us -> none  [the longest x2 8.93 us: backward_move(): center[:, None, :] * field + in_back[:, None, :] * padded[:, 1:-1, :-2]]
    unnamed x101 -> x29, local copies, waits for them, and re-layouts: 20.8 us -> 8.31 us
  transfers between devices with their start and end apart: 19 -> 0, of which waited for: 12 -> 0; matrix products, arithmetic and copies ran while one was open for 18% -> 0% of each run, Pallas kernels for 0% -> 0%
where the time goes in v1:
time: 90.2 us; the launch traced here: 89.7 us
  Pallas kernels  80.1 us (89%)
  local copies, waits for them, and re-layouts  8.83 us (10%)
    pallas_call x1, Pallas kernels, per_device(): pl.pallas_call(kernel, out_shape=(jax.ShapeDtypeStruct(density.shape, F32...  80.1 us
    unnamed x29, local copies, waits for them, and re-layouts  8.31 us

profile of v1, /device:TPU:8, one launch (start us, length us, event | category | flops | bytes accessed | tf_op | source)
XLA Modules:
  0.0 89.7 jit_solution(5351487600461513089)
XLA Ops:
  0.6 0.0 copy-start.11
  0.6 0.0 copy-start.13
  0.7 0.0 copy-start.9
  0.7 0.0 copy-start.10
  0.7 0.0 copy-start.7
  0.7 0.0 copy-start.8
  0.7 0.0 copy-start.12
  0.7 0.6 copy-done.11
  1.3 0.0 copy-done.13
  1.3 0.0 copy-done.9
  1.3 0.0 copy-done.10
  1.4 0.0 copy-done.7
  1.4 0.0 copy-done.8
  1.4 0.0 copy-done.12
  1.4 0.0 copy-start
  1.4 1.2 %copy-done = f32[64,32,128]{2,1,0:T(8,128)S(1)} copy-done((f32[64,32,128]{2,1,0:T(8,128)S(1)}, f32[64,32,128]{2,1,0:T(8,128)}, u32[]{:S(2)}) %copy-start) | copy-done | bytes 1048600
  2.6 0.0 copy-start.1
  2.6 1.2 %copy-done.1 = f32[64,32,128]{2,1,0:T(8,128)S(1)} copy-done((f32[64,32,128]{2,1,0:T(8,128)S(1)}, f32[64,32,128]{2,1,0:T(8,128)}, u32[]{:S(2)}) %copy-start.1) | copy-done | bytes 1048600
  3.8 0.0 copy-start.2
  3.9 0.9 %copy-done.2 = f32[256,256]{1,0:T(8,128)S(1)} copy-done((f32[256,256]{1,0:T(8,128)S(1)}, f32[256,256]{1,0:T(8,128)}, u32[]{:S(2)}) %copy-start.2) | copy-done | bytes 262168
  4.8 0.0 copy-start.3
  4.8 0.9 %copy-done.3 = f32[64,512]{1,0:T(8,128)S(1)} copy-done((f32[64,512]{1,0:T(8,128)S(1)}, f32[64,512]{1,0:T(8,128)}, u32[]{:S(2)}) %copy-start.3) | copy-done | bytes 131096
  5.7 0.0 copy-start.4
  5.7 0.9 %copy-done.4 = f32[64,512]{1,0:T(8,128)S(1)} copy-done((f32[64,512]{1,0:T(8,128)S(1)}, f32[64,512]{1,0:T(8,128)}, u32[]{:S(2)}) %copy-start.4) | copy-done | bytes 131096
  6.6 0.0 copy-start.5
  6.6 0.7 copy-done.5
  7.3 0.0 copy-start.6
  7.3 0.7 copy-done.6
  8.0 80.1 %shard_map.149 = (f32[64,32,128]{2,1,0:T(8,128)S(1)}, f32[8,128]{1,0:T(8,128)S(1)}) custom-call(s32[4,4]{1,0:T(4,128)S(1)} %copy-done.7, f32[64,32,128]{2,1,0:T(8,128)S(1)} %copy-done, f32[64,32,128]{2,1,0:T(8,128)S(1)} %copy-done.1, f32[64,512]{1,0:T(8,128)S(1)} %copy-done.3, f32[64,512]{1,0:T(8,128)S(1)} %copy-done.4, f32[1,64]{1,0:T(1,128)S(1)} %bitcast.12, ...), custom_call_target="tpu_custom_call" | custom-call | tf_op jit(solution)/shard_map/pallas_call | solution.py:513
  88.2 0.5 slice_bitcast_fusion
  88.7 1.0 %copy.17 = f32[64,32,128]{2,1,0:T(8,128)} copy(f32[64,32,128]{2,1,0:T(8,128)S(1)} %get-tuple-element.8) | data formatting | bytes 2097152
Async XLA Ops:
  0.6 0.7 copy-start.11
  0.6 0.7 copy-start.13
  0.7 0.7 copy-start.9
  0.7 0.7 copy-start.10
  0.7 0.7 copy-start.7
  0.7 0.7 copy-start.8
  0.7 0.7 copy-start.12
  1.4 1.2 %copy-start = (f32[64,32,128]{2,1,0:T(8,128)S(1)}, f32[64,32,128]{2,1,0:T(8,128)}, u32[]{:S(2)}) copy-start(f32[64,32,128]{2,1,0:T(8,128)} %density.1) | copy-start | bytes 3145732
  2.6 1.2 %copy-start.1 = (f32[64,32,128]{2,1,0:T(8,128)S(1)}, f32[64,32,128]{2,1,0:T(8,128)}, u32[]{:S(2)}) copy-start(f32[64,32,128]{2,1,0:T(8,128)} %cotangent.1) | copy-start | bytes 3145732
  3.8 0.9 %copy-start.2 = (f32[256,256]{1,0:T(8,128)S(1)}, f32[256,256]{1,0:T(8,128)}, u32[]{:S(2)}) copy-start(f32[256,256]{1,0:T(8,128)} %gain.1) | copy-start | bytes 786436
  4.8 0.9 %copy-start.3 = (f32[64,512]{1,0:T(8,128)S(1)}, f32[64,512]{1,0:T(8,128)}, u32[]{:S(2)}) copy-start(f32[64,512]{1,0:T(8,128)} %drift_in.1) | copy-start | bytes 393220
  5.7 0.9 %copy-start.4 = (f32[64,512]{1,0:T(8,128)S(1)}, f32[64,512]{1,0:T(8,128)}, u32[]{:S(2)}) copy-start(f32[64,512]{1,0:T(8,128)} %drift_out.1) | copy-start | bytes 393220
  6.6 0.7 copy-start.5
  7.3 0.7 copy-start.6

commit v2 on v1

v2 whole, which is shorter than its diff:
```python
import functools

import jax
import jax.numpy as jnp
from jax import lax
from jax.experimental import pallas as pl
from jax.experimental.pallas import tpu as pltpu
from jax.sharding import PartitionSpec as P


MESH = pl.DeviceIdType.MESH
F32 = jnp.float32
BF16 = jnp.bfloat16
RANGE = 64
MASS = 4
ROWS = 8
BINS = 256
LANES = 128
GATE_WIDTH = 0.5
BACK, FORTH = 0, 1
EARLY = 2


def lanes_of(shape):
    return lax.broadcasted_iota(jnp.int32, shape, len(shape) - 1)


def rolled(value, shift):
    shift = shift % LANES
    return value if shift == 0 else pltpu.roll(value, shift, value.ndim - 1)


def swap_blocks(tiles):
    block = lanes_of(tiles[0].shape) // 32
    low = block < 2
    even = block % 2 == 0
    s0, s1, s2, s3 = tiles
    a0 = jnp.where(low, s0, rolled(s2, 64))
    a2 = jnp.where(low, rolled(s0, 64), s2)
    a1 = jnp.where(low, s1, rolled(s3, 64))
    a3 = jnp.where(low, rolled(s1, 64), s3)
    return (
        jnp.where(even, a0, rolled(a1, 32)),
        jnp.where(even, rolled(a0, 96), a1),
        jnp.where(even, a2, rolled(a3, 32)),
        jnp.where(even, rolled(a2, 96), a3),
    )


def high_low(value):
    high = value.astype(BF16)
    return high, (value - high.astype(F32)).astype(BF16)


def kernel(
    pairs_hbm,
    density,
    cotangent,
    drift_in,
    drift_out,
    spread_hbm,
    dest_hbm,
    split_hbm,
    rate_hbm,
    gain_hbm,
    frag_rate_hbm,
    speed_hbm,
    frag_speed_hbm,
    regime_hbm,
    out,
    grad,
    pairs,
    raw_c,
    raw_d,
    in_q,
    out_q,
    spread,
    dest,
    split,
    rate,
    gain,
    frag_rate,
    speed,
    frag_speed,
    regime,
    here,
    own_coef,
    there,
    pack_c,
    pack_d,
    cot,
    m1,
    coef_out,
    coef_in,
    coef,
    back,
    forth,
    gates,
    slopes,
    w2,
    f2,
    a1,
    w1,
    f1,
    st,
    res,
    ret,
    edge_out,
    edge_in,
    acc,
    red,
    load_sem,
    field_send,
    field_recv,
    coef_send,
    coef_recv,
    edge_send,
    edge_recv,
    red_send,
    red_recv,
):
    phi = lax.axis_index("phi")
    row = lax.axis_index("row")
    m = lax.axis_index("mass")
    phis = lax.axis_size("phi")
    rows = lax.axis_size("row")
    low = lax.rem(phi, 8)
    high = phi // 8
    corner = high * MASS + m

    at = pl.multiple_of(row * LANES, LANES)
    sources = (
        (cotangent, raw_c),
        (spread_hbm, spread),
        (drift_in.at[:, pl.ds(at, LANES)], in_q),
        (drift_out.at[:, pl.ds(at, LANES)], out_q),
        (density, raw_d),
        (dest_hbm, dest),
        (split_hbm, split),
        (rate_hbm, rate),
        (gain_hbm, gain),
        (frag_rate_hbm, frag_rate),
        (pairs_hbm, pairs),
        (speed_hbm, speed),
        (frag_speed_hbm, frag_speed),
        (regime_hbm, regime),
    )
    loads = [pltpu.make_async_copy(x, y, load_sem.at[i]) for i, (x, y) in enumerate(sources)]
    for load in loads:
        load.start()

    def mass_peer(k):
        return {"mass": lax.rem(m + k, MASS)}

    def low_peer(k):
        return {"phi": high * 8 + lax.rem(low + k, 8)}

    def corner_peer(k):
        other = lax.rem(corner + k, 8)
        return {"phi": (other // MASS) * 8 + low, "mass": lax.rem(other, MASS)}

    radial = row * MASS + m
    radials = rows * MASS
    right_at = lax.rem(radial + 1, radials)
    left_at = lax.rem(radial + radials - 1, radials)
    right = {"row": right_at // MASS, "mass": lax.rem(right_at, MASS)}
    left = {"row": left_at // MASS, "mass": lax.rem(left_at, MASS)}
    row_right = {"row": lax.rem(row + 1, rows)}
    row_left = {"row": lax.rem(row + rows - 1, rows)}
    after = {"phi": lax.rem(phi + 1, phis)}
    before = {"phi": lax.rem(phi + phis - 1, phis)}

    barrier = pltpu.get_barrier_semaphore()
    greeted = [mass_peer(k) for k in (1, 2, 3)]
    greeted += [right, left, row_right, row_left, after, before]
    greeted += [low_peer(k) for k in range(1, 8)] + [corner_peer(k) for k in range(1, 8)]
    for device in greeted:
        pl.semaphore_signal(barrier, inc=1, device_id=device, device_id_type=MESH)

    tile = (RANGE, LANES)
    lane = lanes_of(tile)
    block = lane // 32
    within = lax.rem(lane, 32)
    first = within == 0
    final = within == 31
    zero = jnp.zeros(tile, F32)

    def field_copy(kind, k, ah, source, target):
        return pltpu.make_async_remote_copy(
            src_ref=source,
            dst_ref=target,
            send_sem=field_send.at[kind, k - 1, ah],
            recv_sem=field_recv.at[kind, k - 1, ah],
            device_id=mass_peer(k),
            device_id_type=MESH,
        )

    own = pl.ds(pl.multiple_of(m * RANGE, RANGE), RANGE)

    def cot_copy(k, ah):
        return field_copy(0, k, ah, pack_c.at[lax.rem(m + k, MASS), ah], cot.at[ah, own])

    def m1_copy(k, ah):
        return field_copy(1, k, ah, pack_d.at[lax.rem(m + k, MASS), ah], m1.at[ah, own])

    def ret_copy(k, ah):
        theirs = pl.ds(pl.multiple_of(lax.rem(m + k, MASS) * RANGE, RANGE), RANGE)
        return field_copy(2, k, ah, res.at[ah, theirs], ret.at[m, ah])

    def coef_copy(k):
        return pltpu.make_async_remote_copy(
            src_ref=coef_out.at[lax.rem(m + k, MASS)],
            dst_ref=coef_in.at[own],
            send_sem=coef_send.at[k - 1],
            recv_sem=coef_recv.at[k - 1],
            device_id=mass_peer(k),
            device_id_type=MESH,
        )

    def edge_copy(n, i):
        device = ((row_right, row_left) if n == 2 else (right, left)) + (after, before)
        return pltpu.make_async_remote_copy(
            src_ref=edge_out.at[n, i],
            dst_ref=edge_in.at[n, i],
            send_sem=edge_send.at[n, i],
            recv_sem=edge_recv.at[n, i],
            device_id=device[i],
            device_id_type=MESH,
        )

    flat_c = raw_c.reshape(RANGE * 32, LANES)

    def send_cot(i, carry):
        ah = lax.rem(i + 7, 8)
        tiles = swap_blocks([flat_c[pl.ds(al * 8 + ah, RANGE, stride=32), :] for al in range(4)])
        for k in range(MASS):
            pack_c[k, ah] = tiles[k]
        for k in (1, 2, 3):
            cot_copy(k, ah).start()
        cot[ah, own] = pack_c[m, ah]
        return carry

    loads[0].wait()
    pl.semaphore_wait(barrier, len(greeted))
    lax.fori_loop(0, ROWS, send_cot, 0)

    for i in (1, 2, 3):
        loads[i].wait()
    square = (RANGE, RANGE)
    on_diag = lax.broadcasted_iota(jnp.int32, square, 0) == lanes_of(square)
    spread_col = jnp.sum(jnp.where(on_diag, jnp.broadcast_to(spread[...], square), 0.0), axis=1, keepdims=True)
    spread_tile = jnp.broadcast_to(spread_col, tile)
    for k in range(MASS):
        coef_out[k] = jnp.where(
            block == 0,
            rolled(in_q[...], -32 * k),
            jnp.where(block == 1, rolled(out_q[...], 32 - 32 * k), spread_tile),
        )
    for k in (1, 2, 3):
        coef_copy(k).start()
    coef_in[own] = coef_out[m]
    own_coef[0] = 1.0 - in_q[...] - out_q[...] - 2.0 * spread_tile
    own_coef[1] = spread_tile

    loads[4].wait()
    flat_d = raw_d.reshape(RANGE * 32, LANES)
    edge_out[2, 2] = flat_d[pl.ds(31, RANGE, stride=32), :]
    edge_out[2, 3] = flat_d[pl.ds(0, RANGE, stride=32), :]
    edge_copy(2, 2).start()
    edge_copy(2, 3).start()
    lowest = lane == 0
    topmost = lane == LANES - 1

    def own_edges(i, carry):
        last_col, first_col = carry
        for k in range(4):
            a = i * 4 + k
            value = flat_d[pl.ds(a, RANGE, stride=32), :]
            here[a + 1] = value
            last_col = jnp.where(topmost, out_q[...] * value, rolled(last_col, -1))
            first_col = jnp.where(lowest, in_q[...] * value, rolled(first_col, 1))
        return last_col, first_col

    last_col, first_col = lax.fori_loop(0, 8, own_edges, (zero, zero))
    edge_out[2, 0] = last_col
    edge_out[2, 1] = first_col
    edge_copy(2, 0).start()
    edge_copy(2, 1).start()

    for load in loads[5:]:
        load.wait()
    whole = (BINS, BINS)
    row_ids = lax.broadcasted_iota(jnp.int32, whole, 0)
    col_ids = lanes_of(whole)
    target = jnp.broadcast_to(dest[...], whole)
    upper = jnp.broadcast_to(split[...], whole)
    diag = jnp.where(row_ids == col_ids, 1.0, 0.0)
    coag_full = (
        jnp.where(row_ids == target, 1.0 - upper, 0.0) + jnp.where(row_ids == target + 1, upper, 0.0) - diag
    ) * rate[...]
    strip = (RANGE, BINS)
    strip_block = lanes_of(strip) // RANGE
    chosen = []
    for i in range(MASS):
        line = jnp.zeros(strip, F32)
        for j in range(MASS):
            line = jnp.where(strip_block == j, pairs[i, j].astype(F32), line)
        chosen.append(line)
    chosen = jnp.concatenate(chosen, axis=0)
    frag_full = gain[...] * chosen * jnp.where(row_ids <= col_ids, 1.0, 0.0) - diag * frag_rate[...]
    for at_row, matrix in ((0, coag_full), (BINS, frag_full)):
        for kept, value in ((forth, matrix), (back, matrix.T)):
            hi, lo = high_low(value)
            kept[at_row : at_row + BINS, 0:BINS] = hi
            kept[at_row : at_row + BINS, BINS : 2 * BINS] = hi
            kept[at_row : at_row + BINS, 2 * BINS : 3 * BINS] = lo

    sigma = 1.0 / (1.0 + jnp.exp(-((speed[...] - frag_speed[...]) / GATE_WIDTH)))
    flagged = regime[...].astype(F32)
    gate_all = flagged * sigma
    slope_all = -flagged * sigma * (1.0 - sigma) / GATE_WIDTH
    block8 = lanes_of((ROWS, LANES)) // 32
    for source, kept in ((gate_all, gates), (slope_all, slopes)):
        value = jnp.zeros((ROWS, LANES), F32)
        for al in range(4):
            part = pltpu.roll(source[al * 8 : al * 8 + 8], lax.rem(32 * (al + MASS - m), LANES), 1)
            value = jnp.where(block8 == al, part, value)
        kept[...] = value

    for i in range(4):
        edge_copy(2, i).wait_recv()
    here[0] = edge_in[2, 2]
    here[33] = edge_in[2, 3]
    row_has_left = jnp.where(row > 0, 1.0, 0.0)
    row_has_right = jnp.where(row < rows - 1, 1.0, 0.0)

    def own_forward(i, carry):
        last_col, first_col = carry
        for k in range(4):
            a = i * 4 + k
            value = here[a + 1]
            beside = here[a] + here[a + 2]
            outer = jnp.where(topmost, first_col, rolled(in_q[...] * value, -1))
            inner = jnp.where(lowest, last_col, rolled(out_q[...] * value, 1))
            there[a] = own_coef[0] * value + outer + inner + own_coef[1] * beside
            last_col = rolled(last_col, -1)
            first_col = rolled(first_col, 1)
        return last_col, first_col

    lax.fori_loop(
        0,
        8,
        own_forward,
        (rolled(edge_in[2, 0], 32) * row_has_left, rolled(edge_in[2, 1], 96) * row_has_right),
    )

    def pack_m1(ah, carry):
        tiles = swap_blocks([there[al * 8 + ah] for al in range(4)])
        for k in range(MASS):
            pack_d[k, ah] = tiles[k]
        m1[ah, own] = pack_d[m, ah]
        return carry

    lax.fori_loop(0, ROWS, pack_m1, 0)

    def send_m1(i, carry):
        for k in (1, 2, 3):
            m1_copy(k, lax.rem(i + 7, 8)).start()
        return carry

    lax.fori_loop(0, EARLY, send_m1, 0)

    has_left = jnp.where(radial > 0, 1.0, 0.0)
    has_right = jnp.where(radial < radials - 1, 1.0, 0.0)

    def mix(n, source, matrix, way, state, arrive, seen):
        edge_out[n, 0] = zero
        edge_out[n, 1] = zero

        def body(j, carry):
            pair = (lax.rem(2 * j + 7, 8), 2 * j)
            for ah in pair:
                arrive(ah)
            x = jnp.concatenate([source[ah] for ah in pair], axis=1)
            x_hi, x_lo = high_low(x)
            y = jnp.dot(matrix[...], jnp.concatenate([x_hi, x_lo, x_hi], axis=0), preferred_element_type=F32)
            gate = jnp.concatenate([gates[pl.ds(ah, 1)] for ah in pair], axis=1)
            new = x + (y[:BINS] + gate * y[BINS:])
            for half, ah in enumerate(pair):
                lanes = slice(half * LANES, (half + 1) * LANES)
                state[ah + 1] = new[:, lanes]
                seen(ah, x[:, lanes], y[BINS:, lanes])
                last_col, first_col = edge_out[n, 0], edge_out[n, 1]
                for g in range(MASS):
                    bins = slice(g * RANGE, (g + 1) * RANGE)
                    value = new[bins, lanes]
                    to_left = value * coef[0, bins] if way == FORTH else value
                    to_right = value * coef[1, bins] if way == FORTH else value
                    last_col = jnp.where(final, to_right, rolled(last_col, -1))
                    first_col = jnp.where(first, to_left, rolled(first_col, 1))
                edge_out[n, 0] = last_col
                edge_out[n, 1] = first_col

            @pl.when(j == 0)
            def _():
                for i, ah in ((2, ROWS), (3, 1)):
                    value = zero
                    for g in range(MASS):
                        bins = slice(g * RANGE, (g + 1) * RANGE)
                        part = rolled(state[ah, bins], 32 * (g - 3) if i == 2 else 32 * g)
                        value = jnp.where(block == g, part, value)
                    edge_out[n, i] = value
                    edge_copy(n, i).start()

            return carry

        lax.fori_loop(0, ROWS // 2, body, 0)
        edge_copy(n, 0).start()
        edge_copy(n, 1).start()

    def stencil(n, field, way, emit, after_row=None):
        edge_copy(n, 0).wait_recv()
        edge_copy(n, 1).wait_recv()

        def body(i, carry):
            last_col, first_col = carry
            ah = lax.rem(14 - i, 8)
            for g in reversed(range(MASS)):
                bins = slice(g * RANGE, (g + 1) * RANGE)
                value = field[ah + 1, bins]
                beside = field[ah, bins] + field[ah + 2, bins]
                c_in, c_out = coef[0, bins], coef[1, bins]
                to_left = c_in * value if way == FORTH else value
                to_right = c_out * value if way == FORTH else value
                outer = rolled(jnp.where(first, first_col, to_left), -1)
                inner = rolled(jnp.where(final, last_col, to_right), 1)
                both = outer + inner if way == FORTH else c_in * inner + c_out * outer
                emit(ah, bins, coef[3, bins] * value + both + coef[2, bins] * beside)
                last_col = rolled(last_col, 1)
                first_col = rolled(first_col, -1)
            if after_row is not None:
                after_row(ah)
            return last_col, first_col

        carry = (rolled(edge_in[n, 0], -32) * has_left, rolled(edge_in[n, 1], 32) * has_right)
        carry = lax.fori_loop(0, 6, body, carry)
        edge_copy(n, 2).wait_recv()
        edge_copy(n, 3).wait_recv()
        for g in range(MASS):
            bins = slice(g * RANGE, (g + 1) * RANGE)
            field[0, bins] = jnp.where(
                block == 0, rolled(edge_in[n, 2], -32 * g), rolled(field[ROWS, bins], 32)
            )
            field[ROWS + 1, bins] = jnp.where(
                block == 3, rolled(edge_in[n, 3], 32 * (3 - g)), rolled(field[1, bins], -32)
            )
        lax.fori_loop(6, 8, body, carry)

    def add_product(ah, value, other):
        summed = jnp.sum((value * other).reshape(-1, 8, LANES), axis=0)
        acc[...] += slopes[pl.ds(ah, 1)] * summed

    def arrived(copy):
        def wait(ah):
            for k in (1, 2, 3):
                copy(k, ah).wait_recv()

        return wait

    acc[...] = jnp.zeros((8, LANES), F32)

    def keep_f2(ah, x, frags):
        f2[ah] = frags

    mix(0, cot, back, BACK, w2, arrived(cot_copy), keep_f2)
    lax.fori_loop(EARLY, ROWS, send_m1, 0)

    for k in (1, 2, 3):
        coef_copy(k).wait_recv()
    for g in range(MASS):
        bins = slice(g * RANGE, (g + 1) * RANGE)
        turns = [rolled(coef_in[bins], 32 * k) for k in range(4)]

        def everywhere(source):
            value = turns[(0 - source) % 4]
            for b in (1, 2, 3):
                value = jnp.where(block == b, turns[(b - source) % 4], value)
            return value

        c_in, c_out, c_spread = everywhere(0), everywhere(1), everywhere(2)
        coef[0, bins] = c_in
        coef[1, bins] = c_out
        coef[2, bins] = c_spread
        coef[3, bins] = 1.0 - c_in - c_out - 2.0 * c_spread

    def keep_a1(ah, bins, value):
        a1[ah, bins] = value

    stencil(0, w2, BACK, keep_a1)

    def keep_f1(ah, x, frags):
        f1[ah] = frags

    mix(1, a1, back, BACK, w1, lambda ah: None, keep_f1)

    def first_product(ah, x, frags):
        add_product(ah, x, f1[ah])

    mix(3, m1, forth, FORTH, st, arrived(m1_copy), first_product)

    def keep_res(ah, bins, value):
        res[ah, bins] = value

    def send_row(ah):
        for k in (1, 2, 3):
            ret_copy(k, ah).start()
        ret[m, ah] = res[ah, own]

    stencil(1, w1, BACK, keep_res, send_row)

    def second_product(ah, bins, value):
        add_product(ah, value, f2[ah, bins])

    stencil(3, st, FORTH, second_product)

    flat_out = out.reshape(RANGE * 32, LANES)

    def unpack(i, carry):
        ah = lax.rem(14 - i, 8)
        arrived(ret_copy)(ah)
        tiles = swap_blocks([ret[k, ah] for k in range(MASS)])
        for al in range(4):
            flat_out[pl.ds(al * 8 + ah, RANGE, stride=32), :] = tiles[al]
        return carry

    total = jnp.sum(acc[...], axis=0, keepdims=True)
    total = total + rolled(total, 32) + rolled(total, 64) + rolled(total, 96)
    total = jnp.broadcast_to(total, (8, LANES))
    total = jnp.where(block8 == m, total, 0.0)
    for n, (place, peer) in enumerate(((low, low_peer), (corner, corner_peer))):
        red[n, place] = total
        copies = []
        for k in range(1, 8):
            copies.append(
                pltpu.make_async_remote_copy(
                    src_ref=red.at[n, place],
                    dst_ref=red.at[n, place],
                    send_sem=red_send.at[n, k - 1],
                    recv_sem=red_recv.at[n, k - 1],
                    device_id=peer(k),
                    device_id_type=MESH,
                )
            )
        for copy in copies:
            copy.start()
        lax.fori_loop(4 * n, 4 * n + 4, unpack, 0)
        for copy in copies:
            copy.wait()
        total = ((red[n, 0] + red[n, 1]) + (red[n, 2] + red[n, 3])) + (
            (red[n, 4] + red[n, 5]) + (red[n, 6] + red[n, 7])
        )
    grad[...] = total[0:1]

    def drain(ah, carry):
        for copy in (cot_copy, m1_copy, ret_copy):
            for k in (1, 2, 3):
                copy(k, ah).wait_send()
        return carry

    lax.fori_loop(0, ROWS, drain, 0)
    for k in (1, 2, 3):
        coef_copy(k).wait_send()
    for n in range(4):
        for i in range(4):
            edge_copy(n, i).wait_send()


def per_device(
    density,
    cotangent,
    drift_in,
    drift_out,
    spread,
    dest_bins,
    bott_split,
    coag_rate,
    frag_pairs,
    frag_gain,
    frag_rate,
    collide_speed,
    frag_speed,
    regime,
):
    vmem = pl.BlockSpec(memory_space=pltpu.VMEM)
    hbm = pl.BlockSpec(memory_space=pltpu.HBM)
    field = pltpu.VMEM((ROWS, BINS, LANES), F32)
    padded = pltpu.VMEM((ROWS + 2, BINS, LANES), F32)
    packed = pltpu.VMEM((MASS, ROWS, RANGE, LANES), F32)
    raw = pltpu.VMEM(density.shape, F32)
    matrix = pltpu.VMEM((2 * BINS, 3 * BINS), BF16)
    small = pltpu.VMEM((ROWS, LANES), F32)
    edges = pltpu.VMEM((4, 4, RANGE, LANES), F32)
    tile = pltpu.VMEM((RANGE, LANES), F32)
    per_bin = pltpu.VMEM((1, BINS), F32)
    cells = pltpu.VMEM((32, LANES), F32)
    dma = pltpu.SemaphoreType.DMA
    adjoint, gradient = pl.pallas_call(
        kernel,
        out_shape=(
            jax.ShapeDtypeStruct(density.shape, F32),
            jax.ShapeDtypeStruct((1, LANES), F32),
        ),
        in_specs=[hbm] * 14,
        out_specs=(vmem, vmem),
        scratch_shapes=[
            pltpu.SMEM((MASS, MASS), jnp.int32),
            raw,
            raw,
            tile,
            tile,
            pltpu.VMEM((1, RANGE), F32),
            pltpu.VMEM((1, BINS), jnp.int32),
            per_bin,
            per_bin,
            pltpu.VMEM((BINS, BINS), F32),
            per_bin,
            cells,
            pltpu.VMEM((1, LANES), F32),
            pltpu.VMEM((32, LANES), jnp.int32),
            pltpu.VMEM((34, RANGE, LANES), F32),
            pltpu.VMEM((2, RANGE, LANES), F32),
            pltpu.VMEM((32, RANGE, LANES), F32),
            packed,
            packed,
            field,
            field,
            pltpu.VMEM((MASS, RANGE, LANES), F32),
            pltpu.VMEM((BINS, LANES), F32),
            pltpu.VMEM((4, BINS, LANES), F32),
            matrix,
            matrix,
            small,
            small,
            padded,
            field,
            field,
            padded,
            field,
            padded,
            field,
            packed,
            edges,
            edges,
            small,
            pltpu.VMEM((2, 8, ROWS, LANES), F32),
            dma((14,)),
            dma((3, 3, ROWS)),
            dma((3, 3, ROWS)),
            dma((3,)),
            dma((3,)),
            dma((4, 4)),
            dma((4, 4)),
            dma((2, 7)),
            dma((2, 7)),
        ],
        compiler_params=pltpu.CompilerParams(
            collective_id=0, has_side_effects=True, vmem_limit_bytes=48 << 20
        ),
    )(
        frag_pairs,
        density,
        cotangent,
        drift_in,
        drift_out,
        spread[None, :],
        dest_bins[None, :],
        bott_split[None, :],
        coag_rate[None, :],
        frag_gain,
        frag_rate[None, :],
        collide_speed,
        frag_speed[None, :],
        regime,
    )
    return adjoint, gradient[0]


def solution(mesh):
    in_specs = (
        P("mass", "phi", "row"),
        P("mass", "phi", "row"),
        P("mass", None),
        P("mass", None),
        P("mass"),
        P(),
        P(),
        P(),
        P(),
        P(),
        P(),
        P("phi", "row"),
        P("row"),
        P("phi", "row"),
    )
    out_specs = (P("mass", "phi", "row"), P("row"))
    return jax.shard_map(
        per_device, mesh=mesh, in_specs=in_specs, out_specs=out_specs, check_vma=False
    )
```

time: 90.2 us -> 66.4 us (0.74)
  Pallas kernels: 80.1 us -> 55.9 us
    pallas_call x1, Pallas kernels: 80.1 us -> 55.9 us  [per_device(): pl.pallas_call(kernel, out_shape=(jax.ShapeDtypeStruct(density.shape, F32...]
    unnamed x29 -> x30, local copies, waits for them, and re-layouts: 8.31 us -> 8.83 us
where the time goes in v2:
time: 66.4 us; the launch traced here: 65.4 us
  Pallas kernels  55.9 us (84%)
  local copies, waits for them, and re-layouts  8.83 us (13%)
  between operations  0.71 us (1%)
    pallas_call x1, Pallas kernels, per_device(): pl.pallas_call(kernel, out_shape=(jax.ShapeDtypeStruct(density.shape, F32...  55.9 us
    unnamed x30, local copies, waits for them, and re-layouts  8.83 us

profile of v2, /device:TPU:8, one launch (start us, length us, event | category | flops | bytes accessed | tf_op | source)
XLA Modules:
  0.0 65.4 jit_solution(17388212681327183848)
XLA Ops:
  0.6 0.0 copy-start.11
  0.6 0.0 copy-start.13
  0.7 0.0 copy-start.9
  0.7 0.0 copy-start.10
  0.7 0.0 copy-start.7
  0.7 0.0 copy-start.8
  0.7 0.0 copy-start.12
  0.7 0.6 copy-done.11
  1.3 0.0 copy-done.13
  1.3 0.0 copy-done.9
  1.3 0.0 copy-done.10
  1.4 0.0 copy-done.7
  1.4 0.0 copy-done.8
  1.4 0.0 copy-done.12
  1.4 0.0 copy-start
  1.4 1.2 %copy-done = f32[64,32,128]{2,1,0:T(8,128)S(1)} copy-done((f32[64,32,128]{2,1,0:T(8,128)S(1)}, f32[64,32,128]{2,1,0:T(8,128)}, u32[]{:S(2)}) %copy-start) | copy-done | bytes 1048600
  2.6 0.0 copy-start.1
  2.6 1.2 %copy-done.1 = f32[64,32,128]{2,1,0:T(8,128)S(1)} copy-done((f32[64,32,128]{2,1,0:T(8,128)S(1)}, f32[64,32,128]{2,1,0:T(8,128)}, u32[]{:S(2)}) %copy-start.1) | copy-done | bytes 1048600
  3.8 0.0 copy-start.2
  3.9 0.9 %copy-done.2 = f32[256,256]{1,0:T(8,128)S(1)} copy-done((f32[256,256]{1,0:T(8,128)S(1)}, f32[256,256]{1,0:T(8,128)}, u32[]{:S(2)}) %copy-start.2) | copy-done | bytes 262168
  4.8 0.0 copy-start.3
  4.8 0.9 %copy-done.3 = f32[64,512]{1,0:T(8,128)S(1)} copy-done((f32[64,512]{1,0:T(8,128)S(1)}, f32[64,512]{1,0:T(8,128)}, u32[]{:S(2)}) %copy-start.3) | copy-done | bytes 131096
  5.7 0.0 copy-start.4
  5.7 0.9 %copy-done.4 = f32[64,512]{1,0:T(8,128)S(1)} copy-done((f32[64,512]{1,0:T(8,128)S(1)}, f32[64,512]{1,0:T(8,128)}, u32[]{:S(2)}) %copy-start.4) | copy-done | bytes 131096
  6.6 0.0 copy-start.5
  6.6 0.7 %copy-done.5 = f32[32,128]{1,0:T(8,128)S(1)} copy-done((f32[32,128]{1,0:T(8,128)S(1)}, f32[32,128]{1,0:T(8,128)}, u32[]{:S(2)}) %copy-start.5) | copy-done | bytes 16408
  7.3 0.0 copy-start.6
  7.3 0.7 %copy-done.6 = s32[32,128]{1,0:T(8,128)S(1)} copy-done((s32[32,128]{1,0:T(8,128)S(1)}, s32[32,128]{1,0:T(8,128)}, u32[]{:S(2)}) %copy-start.6) | copy-done | bytes 16408
  8.0 55.9 %shard_map.149 = (f32[64,32,128]{2,1,0:T(8,128)S(1)}, f32[1,128]{1,0:T(1,128)S(1)}) custom-call(s32[4,4]{1,0:T(4,128)S(1)} %copy-done.7, f32[64,32,128]{2,1,0:T(8,128)S(1)} %copy-done, f32[64,32,128]{2,1,0:T(8,128)S(1)} %copy-done.1, f32[64,512]{1,0:T(8,128)S(1)} %copy-done.3, f32[64,512]{1,0:T(8,128)S(1)} %copy-done.4, f32[1,64]{1,0:T(1,128)S(1)} %bitcast.11, ...), custom_call_target="tpu_custom_call" | custom-call | tf_op jit(solution)/shard_map/pallas_call | solution.py:607
  63.9 1.0 %copy.18 = f32[64,32,128]{2,1,0:T(8,128)} copy(f32[64,32,128]{2,1,0:T(8,128)S(1)} %get-tuple-element.8) | data formatting | bytes 2097152
  64.9 0.5 copy.19
Async XLA Ops:
  0.6 0.7 %copy-start.11 = (f32[256]{0:T(256)S(1)}, f32[256]{0:T(256)}, u32[]{:S(2)}) copy-start(f32[256]{0:T(256)} %param.24) | copy-start | bytes 3076
  0.6 0.7 %copy-start.13 = (f32[128]{0:T(128)S(1)}, f32[128]{0:T(128)}, u32[]{:S(2)}) copy-start(f32[128]{0:T(128)} %param.26) | copy-start | bytes 1540
  0.7 0.7 %copy-start.9 = (f32[256]{0:T(256)S(1)}, f32[256]{0:T(256)}, u32[]{:S(2)}) copy-start(f32[256]{0:T(256)} %param.20) | copy-start | bytes 3076
  0.7 0.7 %copy-start.10 = (f32[256]{0:T(256)S(1)}, f32[256]{0:T(256)}, u32[]{:S(2)}) copy-start(f32[256]{0:T(256)} %param.21) | copy-start | bytes 3076
  0.7 0.7 %copy-start.7 = (s32[4,4]{1,0:T(4,128)S(1)}, s32[4,4]{1,0:T(4,128)}, u32[]{:S(2)}) copy-start(s32[4,4]{1,0:T(4,128)} %pairs_hbm.1) | copy-start | bytes 196
  0.7 0.7 %copy-start.8 = (s32[256]{0:T(256)S(1)}, s32[256]{0:T(256)}, u32[]{:S(2)}) copy-start(s32[256]{0:T(256)} %param.19) | copy-start | bytes 3076
  0.7 0.7 %copy-start.12 = (f32[64]{0:T(128)S(1)}, f32[64]{0:T(128)}, u32[]{:S(2)}) copy-start(f32[64]{0:T(128)} %param.18) | copy-start | bytes 772
  1.4 1.2 %copy-start = (f32[64,32,128]{2,1,0:T(8,128)S(1)}, f32[64,32,128]{2,1,0:T(8,128)}, u32[]{:S(2)}) copy-start(f32[64,32,128]{2,1,0:T(8,128)} %density.1) | copy-start | bytes 3145732
  2.6 1.2 %copy-start.1 = (f32[64,32,128]{2,1,0:T(8,128)S(1)}, f32[64,32,128]{2,1,0:T(8,128)}, u32[]{:S(2)}) copy-start(f32[64,32,128]{2,1,0:T(8,128)} %cotangent.1) | copy-start | bytes 3145732
  3.8 0.9 %copy-start.2 = (f32[256,256]{1,0:T(8,128)S(1)}, f32[256,256]{1,0:T(8,128)}, u32[]{:S(2)}) copy-start(f32[256,256]{1,0:T(8,128)} %gain_hbm.1) | copy-start | bytes 786436
  4.8 0.9 %copy-start.3 = (f32[64,512]{1,0:T(8,128)S(1)}, f32[64,512]{1,0:T(8,128)}, u32[]{:S(2)}) copy-start(f32[64,512]{1,0:T(8,128)} %drift_in.1) | copy-start | bytes 393220
  5.7 0.9 %copy-start.4 = (f32[64,512]{1,0:T(8,128)S(1)}, f32[64,512]{1,0:T(8,128)}, u32[]{:S(2)}) copy-start(f32[64,512]{1,0:T(8,128)} %drift_out.1) | copy-start | bytes 393220
  6.6 0.7 %copy-start.5 = (f32[32,128]{1,0:T(8,128)S(1)}, f32[32,128]{1,0:T(8,128)}, u32[]{:S(2)}) copy-start(f32[32,128]{1,0:T(8,128)} %speed_hbm.1) | copy-start | bytes 49156
  7.3 0.7 %copy-start.6 = (s32[32,128]{1,0:T(8,128)S(1)}, s32[32,128]{1,0:T(8,128)}, u32[]{:S(2)}) copy-start(s32[32,128]{1,0:T(8,128)} %regime_hbm.1) | copy-start | bytes 49156

commit v3 on v2

--- a/solution.py
+++ b/solution.py
@@ -591,6 +591,7 @@
     frag_speed,
     regime,
 ):
+    keep = lambda v: pltpu.with_memory_space_constraint(v, pltpu.HBM)
     vmem = pl.BlockSpec(memory_space=pltpu.VMEM)
     hbm = pl.BlockSpec(memory_space=pltpu.HBM)
     field = pltpu.VMEM((ROWS, BINS, LANES), F32)
@@ -666,22 +667,7 @@
         compiler_params=pltpu.CompilerParams(
             collective_id=0, has_side_effects=True, vmem_limit_bytes=48 << 20
         ),
-    )(
-        frag_pairs,
-        density,
-        cotangent,
-        drift_in,
-        drift_out,
-        spread[None, :],
-        dest_bins[None, :],
-        bott_split[None, :],
-        coag_rate[None, :],
-        frag_gain,
-        frag_rate[None, :],
-        collide_speed,
-        frag_speed[None, :],
-        regime,
-    )
+    )(keep(frag_pairs), keep(density), keep(cotangent), keep(drift_in), keep(drift_out), keep(spread[None, :]), keep(dest_bins[None, :]), keep(bott_split[None, :]), keep(coag_rate[None, :]), keep(frag_gain), keep(frag_rate[None, :]), keep(collide_speed), keep(frag_speed[None, :]), keep(regime))
     return adjoint, gradient[0]
 
 

time: 66.4 us -> 58.7 us (0.88)
  local copies, waits for them, and re-layouts: 8.83 us -> 1.48 us
    unnamed x30 -> x2, local copies, waits for them, and re-layouts: 8.83 us -> 1.48 us
where the time goes in v3:
time: 58.7 us; the launch traced here: 58 us
  Pallas kernels  55.9 us (95%)
  local copies, waits for them, and re-layouts  1.48 us (3%)
  between operations  0.64 us (1%)
    pallas_call x1, Pallas kernels, per_device(): pl.pallas_call(kernel, out_shape=(jax.ShapeDtypeStruct(density.shape, F32...  55.9 us
    unnamed x2, local copies, waits for them, and re-layouts  1.48 us

profile of v3, /device:TPU:8, one launch (start us, length us, event | category | flops | bytes accessed | tf_op | source)
XLA Modules:
  0.0 58.0 jit_solution(15205960780915664231)
XLA Ops:
  0.6 55.9 %shard_map.149 = (f32[64,32,128]{2,1,0:T(8,128)S(1)}, f32[1,128]{1,0:T(1,128)S(1)}) custom-call(s32[4,4]{1,0:T(4,128)} %pairs_hbm.1, f32[64,32,128]{2,1,0:T(8,128)} %density.1, f32[64,32,128]{2,1,0:T(8,128)} %cotangent.1, f32[64,512]{1,0:T(8,128)} %drift_in.1, f32[64,512]{1,0:T(8,128)} %drift_out.1, f32[1,64]{1,0:T(1,128)} %bitcast.12, s32[1,256]{1,0:T(1,128)} %bitcast.8, ...), custom_call_target="tpu_custom_call" | custom-call | tf_op jit(solution)/shard_map/pallas_call | solution.py:608
  56.5 1.0 %copy.18 = f32[64,32,128]{2,1,0:T(8,128)} copy(f32[64,32,128]{2,1,0:T(8,128)S(1)} %get-tuple-element.8) | data formatting | bytes 2097152
  57.5 0.5 copy.19

commit v4 on v3

--- a/solution.py
+++ b/solution.py
@@ -91,7 +91,8 @@
     cot,
     m1,
     coef_out,
-    coef_in,
+    coef_part,
+    coef_all,
     coef,
     back,
     forth,
@@ -114,6 +115,8 @@
     field_recv,
     coef_send,
     coef_recv,
+    share_send,
+    share_recv,
     edge_send,
     edge_recv,
     red_send,
@@ -146,7 +149,7 @@
         (regime_hbm, regime),
     )
     loads = [pltpu.make_async_copy(x, y, load_sem.at[i]) for i, (x, y) in enumerate(sources)]
-    for load in loads:
+    for load in loads[:4]:
         load.start()
 
     def mass_peer(k):
@@ -207,13 +210,25 @@
         theirs = pl.ds(pl.multiple_of(lax.rem(m + k, MASS) * RANGE, RANGE), RANGE)
         return field_copy(2, k, ah, res.at[ah, theirs], ret.at[m, ah])
 
+    eighth = pl.ds(pl.multiple_of(low * 8, 8), 8)
+
     def coef_copy(k):
         return pltpu.make_async_remote_copy(
-            src_ref=coef_out.at[lax.rem(m + k, MASS)],
-            dst_ref=coef_in.at[own],
+            src_ref=coef_out.at[lax.rem(m + k, MASS), eighth],
+            dst_ref=coef_part.at[m],
             send_sem=coef_send.at[k - 1],
             recv_sem=coef_recv.at[k - 1],
             device_id=mass_peer(k),
+            device_id_type=MESH,
+        )
+
+    def share_copy(k):
+        return pltpu.make_async_remote_copy(
+            src_ref=coef_part,
+            dst_ref=coef_all.at[low],
+            send_sem=share_send.at[k - 1],
+            recv_sem=share_recv.at[k - 1],
+            device_id=low_peer(k),
             device_id_type=MESH,
         )
 
@@ -227,22 +242,6 @@
             device_id=device[i],
             device_id_type=MESH,
         )
-
-    flat_c = raw_c.reshape(RANGE * 32, LANES)
-
-    def send_cot(i, carry):
-        ah = lax.rem(i + 7, 8)
-        tiles = swap_blocks([flat_c[pl.ds(al * 8 + ah, RANGE, stride=32), :] for al in range(4)])
-        for k in range(MASS):
-            pack_c[k, ah] = tiles[k]
-        for k in (1, 2, 3):
-            cot_copy(k, ah).start()
-        cot[ah, own] = pack_c[m, ah]
-        return carry
-
-    loads[0].wait()
-    pl.semaphore_wait(barrier, len(greeted))
-    lax.fori_loop(0, ROWS, send_cot, 0)
 
     for i in (1, 2, 3):
         loads[i].wait()
@@ -256,11 +255,29 @@
             rolled(in_q[...], -32 * k),
             jnp.where(block == 1, rolled(out_q[...], 32 - 32 * k), spread_tile),
         )
+    coef_part[m] = coef_out[m, eighth]
+    own_coef[0] = 1.0 - in_q[...] - out_q[...] - 2.0 * spread_tile
+    own_coef[1] = spread_tile
+
+    flat_c = raw_c.reshape(RANGE * 32, LANES)
+
+    def send_cot(i, carry):
+        ah = lax.rem(i + 7, 8)
+        tiles = swap_blocks([flat_c[pl.ds(al * 8 + ah, RANGE, stride=32), :] for al in range(4)])
+        for k in range(MASS):
+            pack_c[k, ah] = tiles[k]
+        for k in (1, 2, 3):
+            cot_copy(k, ah).start()
+        cot[ah, own] = pack_c[m, ah]
+        return carry
+
+    loads[0].wait()
+    for load in loads[4:]:
+        load.start()
+    pl.semaphore_wait(barrier, len(greeted))
     for k in (1, 2, 3):
         coef_copy(k).start()
-    coef_in[own] = coef_out[m]
-    own_coef[0] = 1.0 - in_q[...] - out_q[...] - 2.0 * spread_tile
-    own_coef[1] = spread_tile
+    lax.fori_loop(0, ROWS, send_cot, 0)
 
     loads[4].wait()
     flat_d = raw_d.reshape(RANGE * 32, LANES)
@@ -272,13 +289,13 @@
     topmost = lane == LANES - 1
 
     def own_edges(i, carry):
-        last_col, first_col = carry
+        last_col, first_col = rolled(carry[0], -4), rolled(carry[1], 4)
         for k in range(4):
             a = i * 4 + k
             value = flat_d[pl.ds(a, RANGE, stride=32), :]
             here[a + 1] = value
-            last_col = jnp.where(topmost, out_q[...] * value, rolled(last_col, -1))
-            first_col = jnp.where(lowest, in_q[...] * value, rolled(first_col, 1))
+            last_col = jnp.where(lane == LANES - 4 + k, rolled(out_q[...] * value, k - 3), last_col)
+            first_col = jnp.where(lane == 3 - k, rolled(in_q[...] * value, 3 - k), first_col)
         return last_col, first_col
 
     last_col, first_col = lax.fori_loop(0, 8, own_edges, (zero, zero))
@@ -286,6 +303,11 @@
     edge_out[2, 1] = first_col
     edge_copy(2, 0).start()
     edge_copy(2, 1).start()
+    for k in (1, 2, 3):
+        coef_copy(k).wait_recv()
+    for k in range(1, 8):
+        share_copy(k).start()
+    coef_all[low] = coef_part[...]
 
     for load in loads[5:]:
         load.wait()
@@ -340,12 +362,10 @@
             a = i * 4 + k
             value = here[a + 1]
             beside = here[a] + here[a + 2]
-            outer = jnp.where(topmost, first_col, rolled(in_q[...] * value, -1))
-            inner = jnp.where(lowest, last_col, rolled(out_q[...] * value, 1))
+            outer = jnp.where(topmost, rolled(first_col, k), rolled(in_q[...] * value, -1))
+            inner = jnp.where(lowest, rolled(last_col, -k), rolled(out_q[...] * value, 1))
             there[a] = own_coef[0] * value + outer + inner + own_coef[1] * beside
-            last_col = rolled(last_col, -1)
-            first_col = rolled(first_col, 1)
-        return last_col, first_col
+        return rolled(last_col, -4), rolled(first_col, 4)
 
     lax.fori_loop(
         0,
@@ -383,23 +403,33 @@
                 arrive(ah)
             x = jnp.concatenate([source[ah] for ah in pair], axis=1)
             x_hi, x_lo = high_low(x)
-            y = jnp.dot(matrix[...], jnp.concatenate([x_hi, x_lo, x_hi], axis=0), preferred_element_type=F32)
+            xc = jnp.concatenate([x_hi, x_lo, x_hi], axis=0)
             gate = jnp.concatenate([gates[pl.ds(ah, 1)] for ah in pair], axis=1)
-            new = x + (y[:BINS] + gate * y[BINS:])
+            news = []
+            yfs = []
+            for c in range(2):
+                part = slice(c * 128, c * 128 + 128)
+                yf = jnp.dot(matrix[BINS + c * 128 : BINS + c * 128 + 128], xc, preferred_element_type=F32)
+                news.append(x[part] + jnp.dot(matrix[part], xc, preferred_element_type=F32) + gate * yf)
+                yfs.append(yf)
+            new = jnp.concatenate(news, axis=0)
+            frags = jnp.concatenate(yfs, axis=0)
+            last_col = rolled(edge_out[n, 0], -8)
+            first_col = rolled(edge_out[n, 1], 8)
             for half, ah in enumerate(pair):
                 lanes = slice(half * LANES, (half + 1) * LANES)
                 state[ah + 1] = new[:, lanes]
-                seen(ah, x[:, lanes], y[BINS:, lanes])
-                last_col, first_col = edge_out[n, 0], edge_out[n, 1]
+                seen(ah, x[:, lanes], frags[:, lanes])
                 for g in range(MASS):
                     bins = slice(g * RANGE, (g + 1) * RANGE)
                     value = new[bins, lanes]
                     to_left = value * coef[0, bins] if way == FORTH else value
                     to_right = value * coef[1, bins] if way == FORTH else value
-                    last_col = jnp.where(final, to_right, rolled(last_col, -1))
-                    first_col = jnp.where(first, to_left, rolled(first_col, 1))
-                edge_out[n, 0] = last_col
-                edge_out[n, 1] = first_col
+                    u = half * MASS + g
+                    last_col = jnp.where(within == 24 + u, rolled(to_right, u - 7), last_col)
+                    first_col = jnp.where(within == 7 - u, rolled(to_left, 7 - u), first_col)
+            edge_out[n, 0] = last_col
+            edge_out[n, 1] = first_col
 
             @pl.when(j == 0)
             def _():
@@ -425,25 +455,26 @@
         def body(i, carry):
             last_col, first_col = carry
             ah = lax.rem(14 - i, 8)
-            for g in reversed(range(MASS)):
+            for t in range(MASS):
+                g = MASS - 1 - t
                 bins = slice(g * RANGE, (g + 1) * RANGE)
                 value = field[ah + 1, bins]
                 beside = field[ah, bins] + field[ah + 2, bins]
                 c_in, c_out = coef[0, bins], coef[1, bins]
                 to_left = c_in * value if way == FORTH else value
                 to_right = c_out * value if way == FORTH else value
-                outer = rolled(jnp.where(first, first_col, to_left), -1)
-                inner = rolled(jnp.where(final, last_col, to_right), 1)
+                outer = rolled(jnp.where(first, rolled(first_col, -t), to_left), -1)
+                inner = rolled(jnp.where(final, rolled(last_col, t), to_right), 1)
                 both = outer + inner if way == FORTH else c_in * inner + c_out * outer
                 emit(ah, bins, coef[3, bins] * value + both + coef[2, bins] * beside)
-                last_col = rolled(last_col, 1)
-                first_col = rolled(first_col, -1)
+            last_col = rolled(last_col, MASS)
+            first_col = rolled(first_col, -MASS)
             if after_row is not None:
                 after_row(ah)
             return last_col, first_col
 
         carry = (rolled(edge_in[n, 0], -32) * has_left, rolled(edge_in[n, 1], 32) * has_right)
-        carry = lax.fori_loop(0, 6, body, carry)
+        carry = lax.fori_loop(0, 6, body, carry, unroll=2)
         edge_copy(n, 2).wait_recv()
         edge_copy(n, 3).wait_recv()
         for g in range(MASS):
@@ -454,7 +485,7 @@
             field[ROWS + 1, bins] = jnp.where(
                 block == 3, rolled(edge_in[n, 3], 32 * (3 - g)), rolled(field[1, bins], -32)
             )
-        lax.fori_loop(6, 8, body, carry)
+        lax.fori_loop(6, 8, body, carry, unroll=True)
 
     def add_product(ah, value, other):
         summed = jnp.sum((value * other).reshape(-1, 8, LANES), axis=0)
@@ -475,11 +506,12 @@
     mix(0, cot, back, BACK, w2, arrived(cot_copy), keep_f2)
     lax.fori_loop(EARLY, ROWS, send_m1, 0)
 
-    for k in (1, 2, 3):
-        coef_copy(k).wait_recv()
+    for k in range(1, 8):
+        share_copy(k).wait_recv()
     for g in range(MASS):
         bins = slice(g * RANGE, (g + 1) * RANGE)
-        turns = [rolled(coef_in[bins], 32 * k) for k in range(4)]
+        sent = jnp.concatenate([coef_all[i, g] for i in range(8)], axis=0)
+        turns = [rolled(sent, 32 * k) for k in range(4)]
 
         def everywhere(source):
             value = turns[(0 - source) % 4]
@@ -570,6 +602,8 @@
     lax.fori_loop(0, ROWS, drain, 0)
     for k in (1, 2, 3):
         coef_copy(k).wait_send()
+    for k in range(1, 8):
+        share_copy(k).wait_send()
     for n in range(4):
         for i in range(4):
             edge_copy(n, i).wait_send()
@@ -636,7 +670,8 @@
             field,
             field,
             pltpu.VMEM((MASS, RANGE, LANES), F32),
-            pltpu.VMEM((BINS, LANES), F32),
+            pltpu.VMEM((MASS, 8, LANES), F32),
+            pltpu.VMEM((8, MASS, 8, LANES), F32),
             pltpu.VMEM((4, BINS, LANES), F32),
             matrix,
             matrix,
@@ -659,6 +694,8 @@
             dma((3, 3, ROWS)),
             dma((3,)),
             dma((3,)),
+            dma((7,)),
+            dma((7,)),
             dma((4, 4)),
             dma((4, 4)),
             dma((2, 7)),

time: 58.7 us -> 57.1 us (0.973)
  Pallas kernels: 55.9 us -> 54.7 us
    pallas_call x1, Pallas kernels: 55.9 us -> 54.7 us  [per_device(): pl.pallas_call(kernel, out_shape=(jax.ShapeDtypeStruct(density.shape, F32...]
where the time goes in v4:
time: 57.1 us; the launch traced here: 56.8 us
  Pallas kernels  54.7 us (96%)
  local copies, waits for them, and re-layouts  1.48 us (3%)
  between operations  0.64 us (1%)
    pallas_call x1, Pallas kernels, per_device(): pl.pallas_call(kernel, out_shape=(jax.ShapeDtypeStruct(density.shape, F32...  54.7 us
    unnamed x2, local copies, waits for them, and re-layouts  1.48 us

profile of v4, /device:TPU:8, one launch (start us, length us, event | category | flops | bytes accessed | tf_op | source)
XLA Modules:
  0.0 56.8 jit_solution(13149162041571943317)
XLA Ops:
  0.6 54.7 %shard_map.149 = (f32[64,32,128]{2,1,0:T(8,128)S(1)}, f32[1,128]{1,0:T(1,128)S(1)}) custom-call(s32[4,4]{1,0:T(4,128)} %pairs_hbm.1, f32[64,32,128]{2,1,0:T(8,128)} %density.1, f32[64,32,128]{2,1,0:T(8,128)} %cotangent.1, f32[64,512]{1,0:T(8,128)} %drift_in.1, f32[64,512]{1,0:T(8,128)} %drift_out.1, f32[1,64]{1,0:T(1,128)} %bitcast.12, s32[1,256]{1,0:T(1,128)} %bitcast.8, ...), custom_call_target="tpu_custom_call" | custom-call | tf_op jit(solution)/shard_map/pallas_call | solution.py:642
  55.3 1.0 %copy.18 = f32[64,32,128]{2,1,0:T(8,128)} copy(f32[64,32,128]{2,1,0:T(8,128)S(1)} %get-tuple-element.8) | data formatting | bytes 2097152
  56.3 0.5 copy.19

commit v5 on v4

--- a/solution.py
+++ b/solution.py
@@ -474,7 +474,7 @@
             return last_col, first_col
 
         carry = (rolled(edge_in[n, 0], -32) * has_left, rolled(edge_in[n, 1], 32) * has_right)
-        carry = lax.fori_loop(0, 6, body, carry, unroll=2)
+        carry = lax.fori_loop(0, 6, body, carry)
         edge_copy(n, 2).wait_recv()
         edge_copy(n, 3).wait_recv()
         for g in range(MASS):
@@ -485,7 +485,7 @@
             field[ROWS + 1, bins] = jnp.where(
                 block == 3, rolled(edge_in[n, 3], 32 * (3 - g)), rolled(field[1, bins], -32)
             )
-        lax.fori_loop(6, 8, body, carry, unroll=True)
+        lax.fori_loop(6, 8, body, carry)
 
     def add_product(ah, value, other):
         summed = jnp.sum((value * other).reshape(-1, 8, LANES), axis=0)

time: 57.1 us -> 55.7 us (0.975)
  Pallas kernels: 54.7 us -> 53.4 us
    pallas_call x1, Pallas kernels: 54.7 us -> 53.4 us  [per_device(): pl.pallas_call(kernel, out_shape=(jax.ShapeDtypeStruct(density.shape, F32...]
where the time goes in v5:
time: 55.7 us; the launch traced here: 55.6 us
  Pallas kernels  53.4 us (96%)
  local copies, waits for them, and re-layouts  1.48 us (3%)
  between operations  0.64 us (1%)
    pallas_call x1, Pallas kernels, per_device(): pl.pallas_call(kernel, out_shape=(jax.ShapeDtypeStruct(density.shape, F32...  53.4 us
    unnamed x2, local copies, waits for them, and re-layouts  1.48 us

profile of v5, /device:TPU:8, one launch (start us, length us, event | category | flops | bytes accessed | tf_op | source)
XLA Modules:
  0.0 55.6 jit_solution(9730331374164700654)
XLA Ops:
  0.6 53.4 %shard_map.149 = (f32[64,32,128]{2,1,0:T(8,128)S(1)}, f32[1,128]{1,0:T(1,128)S(1)}) custom-call(s32[4,4]{1,0:T(4,128)} %pairs_hbm.1, f32[64,32,128]{2,1,0:T(8,128)} %density.1, f32[64,32,128]{2,1,0:T(8,128)} %cotangent.1, f32[64,512]{1,0:T(8,128)} %drift_in.1, f32[64,512]{1,0:T(8,128)} %drift_out.1, f32[1,64]{1,0:T(1,128)} %bitcast.12, s32[1,256]{1,0:T(1,128)} %bitcast.8, ...), custom_call_target="tpu_custom_call" | custom-call | tf_op jit(solution)/shard_map/pallas_call | solution.py:642
  54.1 1.0 %copy.18 = f32[64,32,128]{2,1,0:T(8,128)} copy(f32[64,32,128]{2,1,0:T(8,128)S(1)} %get-tuple-element.8) | data formatting | bytes 2097152
  55.1 0.5 copy.19

commit v6 on v5

--- a/solution.py
+++ b/solution.py
@@ -536,7 +536,9 @@
     mix(1, a1, back, BACK, w1, lambda ah: None, keep_f1)
 
     def first_product(ah, x, frags):
-        add_product(ah, x, f1[ah])
+        @pl.when(jnp.logical_and(ah != 5, ah != 6))
+        def _():
+            add_product(ah, x, f1[ah])
 
     mix(3, m1, forth, FORTH, st, arrived(m1_copy), first_product)
 
@@ -549,6 +551,9 @@
         ret[m, ah] = res[ah, own]
 
     stencil(1, w1, BACK, keep_res, send_row)
+
+    for ah in (5, 6):
+        add_product(ah, m1[ah], f1[ah])
 
     def second_product(ah, bins, value):
         add_product(ah, value, f2[ah, bins])

time: 55.7 us -> 56.6 us (1.016)
  no operation moved by 1% of the time
where the time goes in v6:
time: 56.6 us; the launch traced here: 56 us
  Pallas kernels  53.8 us (95%)
  local copies, waits for them, and re-layouts  1.48 us (3%)
  between operations  0.64 us (1%)
    pallas_call x1, Pallas kernels, per_device(): pl.pallas_call(kernel, out_shape=(jax.ShapeDtypeStruct(density.shape, F32...  53.8 us
    unnamed x2, local copies, waits for them, and re-layouts  1.48 us

profile of v6, /device:TPU:8, one launch (start us, length us, event | category | flops | bytes accessed | tf_op | source)
XLA Modules:
  0.0 56.0 jit_solution(268534197088102228)
XLA Ops:
  0.6 53.8 %shard_map.149 = (f32[64,32,128]{2,1,0:T(8,128)S(1)}, f32[1,128]{1,0:T(1,128)S(1)}) custom-call(s32[4,4]{1,0:T(4,128)} %pairs_hbm.1, f32[64,32,128]{2,1,0:T(8,128)} %density.1, f32[64,32,128]{2,1,0:T(8,128)} %cotangent.1, f32[64,512]{1,0:T(8,128)} %drift_in.1, f32[64,512]{1,0:T(8,128)} %drift_out.1, f32[1,64]{1,0:T(1,128)} %bitcast.12, s32[1,256]{1,0:T(1,128)} %bitcast.8, ...), custom_call_target="tpu_custom_call" | custom-call | tf_op jit(solution)/shard_map/pallas_call | solution.py:647
  54.5 1.0 %copy.18 = f32[64,32,128]{2,1,0:T(8,128)} copy(f32[64,32,128]{2,1,0:T(8,128)S(1)} %get-tuple-element.8) | data formatting | bytes 2097152
  55.4 0.5 copy.19
